TPU v7x, 256 devices: a whole 4x4x8 slice. The times are simulated.
256 devices in a mesh: gx: 8 (over x, core), gy: 4 (over z_lo), gz: 8 (over y, z_hi).
Axes of the slice: x: 4, y: 4, z: 8 (z_hi: 2, z_lo: 4; z = z_hi * 4 + z_lo), core: 2. Of those that a mesh axis runs over, the one named last changes fastest.
Arguments:
- start_block: float32 [32, 3, 2, 8, 16, 1024], P(None, None, None, 'gx', 'gy', 'gz'), may hold values from -700 to 700
- pair_blocks: float32 [3, 3, 16, 2, 8, 16, 1024], P(None, None, None, None, 'gx', 'gy', 'gz'), may hold values from -8 to 8, as said below
- slot_map: int32 [16, 2, 8, 16, 1024], P(None, None, 'gx', 'gy', 'gz'), may hold values from 0 to 15, as said below
Outputs:
- alpha1: float32 [32, 32], replicated
- alpha2: float32 [32, 32], replicated
- beta1: float32 [32, 32], replicated
- beta2: float32 [32, 32], replicated
- basis3: float32 [32, 3, 2, 8, 16, 1024], P(None, None, None, 'gx', 'gy', 'gz')
Inputs may be any that keep to these rules, and one draw needn't show every extreme that they name: `slot_map`: for every atom the 16 slots hold each of 0 to 15 once; 0 to 13 name the neighbour directions of the steps, 14 and 15 mark padding slots. `pair_blocks`: the block an atom holds toward a neighbour is the transpose of the block that neighbour holds toward the atom, so H is symmetric.
All inputs are finite; a program needn't handle non-finite values.
Results may differ from a plain program's by a relative error of at most 0.0003.
Values sent between devices are 32-bit elements; how exact they have to be, the bound alone decides.
A program may use at most 64 MiB of HBM per device.

v0:
```python
import jax
import jax.numpy as jnp
from jax import lax
from jax.sharding import PartitionSpec as P

PRECISE = lax.Precision.HIGHEST


def extended(block, sides, width):
    for axis, dim in sides:
        count = lax.axis_size(axis)
        forward = [(i, i + 1) for i in range(count - 1)]
        forward.append((count - 1, 0))
        backward = [(target, source) for source, target in forward]
        low = lax.ppermute(
            lax.slice_in_dim(block, block.shape[dim] - width, None, axis=dim), axis, forward
        )
        high = lax.ppermute(lax.slice_in_dim(block, 0, width, axis=dim), axis, backward)
        block = jnp.concatenate([low, block, high], axis=dim)
    return block


def neighbour_offset(sublattice, offset_id):
    if offset_id < 8:
        corner_bits = (offset_id >> 2 & 1, offset_id >> 1 & 1, offset_id & 1)
        if sublattice == 0:
            return ((-corner_bits[0], -corner_bits[1], -corner_bits[2]), 1)
        return (corner_bits, 0)
    axis_id = (offset_id - 8) // 2
    direction = 1 if (offset_id - 8) % 2 == 0 else -1
    displacement = tuple((direction if axis_number == axis_id else 0 for axis_number in range(3)))
    return (displacement, sublattice)


def offset_blocks(pair_blocks, slot_map):
    result = []
    for offset_id in range(14):
        chosen = slot_map[None, None] == offset_id
        result.append(jnp.sum(jnp.where(chosen, pair_blocks, jnp.float32(0.0)), axis=2))
    return result


def onsite_blocks(blocks):
    result = []
    for sublattice in range(2):
        onsite = jnp.zeros(blocks[0].shape[:2] + blocks[0].shape[3:], jnp.float32)
        for offset_id in range(14):
            coupling = blocks[offset_id][:, :, sublattice]
            onsite = onsite + 0.5 * (coupling + jnp.swapaxes(coupling, 0, 1))
        result.append(onsite)
    return result


def apply_hessian(vectors, blocks, onsite):
    padded = extended(vectors, (("gx", 3), ("gy", 4), ("gz", 5)), 1)
    size_x, size_y, size_z = (vectors.shape[3], vectors.shape[4], vectors.shape[5])
    outputs = []
    for sublattice in range(2):
        summed = jnp.zeros(vectors.shape[:2] + vectors.shape[3:], jnp.float32)
        for offset_id in range(14):
            displacement, source = neighbour_offset(sublattice, offset_id)
            start_x = 1 + displacement[0]
            start_y = 1 + displacement[1]
            start_z = 1 + displacement[2]
            neighbour = padded[
                :,
                :,
                source,
                start_x : start_x + size_x,
                start_y : start_y + size_y,
                start_z : start_z + size_z,
            ]
            coupling = blocks[offset_id][:, :, sublattice]
            summed = summed + jnp.sum(coupling[None] * neighbour[:, None], axis=2)
        summed = summed - jnp.sum(
            onsite[sublattice][None] * vectors[:, None, :, sublattice], axis=2
        )
        outputs.append(summed)
    return jnp.stack(outputs, axis=2)


def local_gram(left, right):
    left_flat = left.reshape(left.shape[0], -1)
    right_flat = right.reshape(right.shape[0], -1)
    return lax.dot_general(left_flat, right_flat, (((1,), (1,)), ((), ())), precision=PRECISE)


def combine(matrix, vectors):
    flat = vectors.reshape(vectors.shape[0], -1)
    return jnp.dot(matrix, flat, precision=PRECISE).reshape(vectors.shape)


def inverse_factor(gram_matrix):
    lower = jnp.linalg.cholesky(gram_matrix)
    identity = jnp.eye(gram_matrix.shape[0], dtype=gram_matrix.dtype)
    inverse = jax.scipy.linalg.solve_triangular(lower, identity, lower=True)
    return (lower, inverse)


def lanczos_step(basis, image, previous, coupling_prev, row_count):
    alpha = lax.psum(local_gram(image, basis), ("gx", "gy", "gz")) / row_count
    residual = image - combine(alpha, basis)
    if previous is not None:
        residual = residual - combine(coupling_prev.T, previous)
    residual_gram = lax.psum(local_gram(residual, residual), ("gx", "gy", "gz")) / row_count
    return (alpha, residual, residual_gram)


def local(start_block, pair_blocks, slot_map):
    device_count = lax.axis_size("gx") * lax.axis_size("gy") * lax.axis_size("gz")
    row_count = start_block[0].size * device_count
    blocks = offset_blocks(pair_blocks, slot_map)
    onsite = onsite_blocks(blocks)
    start_gram = lax.psum(local_gram(start_block, start_block), ("gx", "gy", "gz")) / row_count
    lower0, inverse0 = inverse_factor(start_gram)
    basis1 = combine(inverse0, start_block)
    image1 = apply_hessian(basis1, blocks, onsite)
    alpha1, residual1, gram_first = lanczos_step(basis1, image1, None, None, row_count)
    beta1, inverse1 = inverse_factor(gram_first)
    basis2 = combine(inverse1, residual1)
    image2 = apply_hessian(basis2, blocks, onsite)
    alpha2, residual2, gram_second = lanczos_step(basis2, image2, basis1, beta1, row_count)
    beta2, inverse2 = inverse_factor(gram_second)
    basis3 = combine(inverse2, residual2)
    return (alpha1, alpha2, beta1, beta2, basis3)


def solution(mesh):
    in_specs = (
        P(None, None, None, "gx", "gy", "gz"),
        P(None, None, None, None, "gx", "gy", "gz"),
        P(None, None, "gx", "gy", "gz"),
    )
    out_specs = (P(), P(), P(), P(), P(None, None, None, "gx", "gy", "gz"))
    return jax.shard_map(local, mesh=mesh, in_specs=in_specs, out_specs=out_specs, check_vma=False)
```

profile of v0, /device:TPU:32, one launch (start us, length us, event | category | flops | bytes accessed | tf_op | source)
XLA Modules:
  0.0 520.9 jit_solution(3226206658296597986)
XLA Ops:
  3.4 79.9 %psum.35 = f32[32,32]{0,1:T(8,128)S(1)} all-reduce(f32[32,32]{0,1:T(8,128)S(1)} %convolution_bitcast_fusion.2), channel_id=1, replica_groups=mesh['gx'=8,'gy'=4,'gz'=8] {'gx','gy','gz'}, use_global_device_ids=true, to_apply=%region_1.2 | all-reduce | flops 1024 | bytes 8192 | tf_op jit(solution)/shard_map/psum | solution.py:114
  83.4 2.9 cholesky.59
  87.7 2.4 custom-call.7
  91.2 2.9 collective-permute-start.1
  94.5 2.5 select_reduce_fusion.13
  106.2 2.0 collective-permute-start.3
  111.4 4.4 collective-permute-done.2
  115.9 3.2 collective-permute-done.3
  120.0 1.8 fusion.52
  121.9 2.8 copy.507
  124.7 4.6 collective-permute-start.5
  133.6 2.7 copy.419
  136.3 4.8 collective-permute-done.4
  149.9 74.7 %psum.36 = f32[32,32]{0,1:T(8,128)S(1)} all-reduce(f32[32,32]{0,1:T(8,128)S(1)} %fusion.56), channel_id=1, replica_groups=mesh['gx'=8,'gy'=4,'gz'=8] {'gx','gy','gz'}, use_global_device_ids=true, to_apply=%region_47.50 | all-reduce | flops 1024 | bytes 8192 | tf_op jit(solution)/shard_map/psum | solution.py:101
  225.6 73.1 %psum.37 = f32[32,32]{0,1:T(8,128)S(1)} all-reduce(f32[32,32]{0,1:T(8,128)S(1)} %fusion.57), channel_id=1, replica_groups=mesh['gx'=8,'gy'=4,'gz'=8] {'gx','gy','gz'}, use_global_device_ids=true, to_apply=%region_48.51 | all-reduce | flops 1024 | bytes 8192 | tf_op jit(solution)/shard_map/psum | solution.py:105
  298.7 2.9 cholesky.70
  303.0 2.4 custom-call.8
  306.5 2.9 collective-permute-start.7
  312.0 2.9 collective-permute-done.6
  315.2 2.0 collective-permute-start.9
  319.8 5.3 %collective-permute-done.8 = f32[32,3,2,3,1,128]{5,0,4,3,2,1:T(8,128)S(1)} collective-permute-done((f32[32,3,2,3,1,128]{5,0,4,3,2,1:T(8,128)S(1)}, f32[32,3,2,3,1,128]{5,0,4,3,2,1:T(8,128)S(1)}, u32[]{:S(2)}, u32[]{:S(2)}) %collective-permute-start.8) | collective-permute-done | bytes 294944 | tf_op jit(solution)/shard_map/ppermute | solution.py:15
  325.1 5.3 %collective-permute-done.9 = f32[32,3,2,3,1,128]{5,0,4,3,2,1:T(8,128)S(1)} collective-permute-done((f32[32,3,2,3,1,128]{5,0,4,3,2,1:T(8,128)S(1)}, f32[32,3,2,3,1,128]{5,0,4,3,2,1:T(8,128)S(1)}, u32[]{:S(2)}, u32[]{:S(2)}) %collective-permute-start.9) | collective-permute-done | bytes 294944 | tf_op jit(solution)/shard_map/ppermute | solution.py:18
  331.3 1.8 fusion.51
  333.2 2.8 copy.509
  336.0 4.0 collective-permute-start.11
  342.8 1.9 collective-permute-start.10
  346.3 2.2 maximum_bitcast_fusion.4
  349.4 3.9 collective-permute-done.10
  362.0 74.9 %psum.38 = f32[32,32]{0,1:T(8,128)S(1)} all-reduce(f32[32,32]{0,1:T(8,128)S(1)} %fusion.59), channel_id=1, replica_groups=mesh['gx'=8,'gy'=4,'gz'=8] {'gx','gy','gz'}, use_global_device_ids=true, to_apply=%region_79.82 | all-reduce | flops 1024 | bytes 8192 | tf_op jit(solution)/shard_map/psum | solution.py:101
  438.6 72.5 %psum.39 = f32[32,32]{0,1:T(8,128)S(1)} all-reduce(f32[32,32]{0,1:T(8,128)S(1)} %fusion.60), channel_id=1, replica_groups=mesh['gx'=8,'gy'=4,'gz'=8] {'gx','gy','gz'}, use_global_device_ids=true, to_apply=%region_80.83 | all-reduce | flops 1024 | bytes 8192 | tf_op jit(solution)/shard_map/psum | solution.py:105
  511.2 2.9 cholesky.81
  516.1 2.4 custom-call.9
  (353 shorter events, 60.4 us)
Async XLA Ops:
  3.4 90.7 %copy-start.95 = (s32[16,2,1,4,128]{4,3,2,1,0:T(4,128)S(1)}, s32[16,2,1,4,128]{4,3,2,1,0:T(4,128)}, u32[]{:S(2)}) copy-start(s32[16,2,1,4,128]{4,3,2,1,0:T(4,128)} %param.8) | copy-start | bytes 196612
  87.0 7.5 %copy-start.35 = (f32[3,3,16,2,1,4,128]{6,5,4,3,2,1,0:T(4,128)S(1)}, f32[3,3,16,2,1,4,128]{6,5,4,3,2,1,0:T(4,128)}, u32[]{:S(2)}) copy-start(f32[3,3,16,2,1,4,128]{6,5,4,3,2,1,0:T(4,128)} %param.7) | copy-start | bytes 1769476
  91.1 14.8 %collective-permute-start = (f32[32,3,2,1,4,128]{5,0,4,3,2,1:T(8,128)S(1)}, f32[32,3,2,1,4,128]{5,0,4,3,2,1:T(8,128)S(1)}, u32[]{:S(2)}, u32[]{:S(2)}) collective-permute-start(f32[32,3,2,1,4,128]{5,0,4,3,2,1:T(8,128)S(1)} %copy.391), channel_id=1, source_target_pairs={{0,32},{32,64},{64,96},{96,128},{128,160},{160,192},{192,224},{224... | collective-permute-start | bytes 1179656 | tf_op jit(solution)/shard_map/ppermute | solution.py:15
  91.2 14.9 %collective-permute-start.1 = (f32[32,3,2,1,4,128]{5,0,4,3,2,1:T(8,128)S(1)}, f32[32,3,2,1,4,128]{5,0,4,3,2,1:T(8,128)S(1)}, u32[]{:S(2)}, u32[]{:S(2)}) collective-permute-start(f32[32,3,2,1,4,128]{5,0,4,3,2,1:T(8,128)S(1)} %copy.391), channel_id=1, source_target_pairs={{32,0},{64,32},{96,64},{128,96},{160,128},{192,160},{224,192},{0,2... | collective-permute-start | bytes 1179656 | tf_op jit(solution)/shard_map/ppermute | solution.py:18
  100.2 8.7 %copy-start.84 = (f32[3,3,4,128]{3,2,0,1:T(4,128)}, f32[3,3,4,128]{3,2,0,1:T(4,128)S(1)}, u32[]{:S(2)}) copy-start(f32[3,3,4,128]{3,2,0,1:T(4,128)S(1)} %get-tuple-element.159) | copy-start | bytes 55300
  100.3 9.4 %copy-start.82 = (f32[3,3,4,128]{3,2,0,1:T(4,128)}, f32[3,3,4,128]{3,2,0,1:T(4,128)S(1)}, u32[]{:S(2)}) copy-start(f32[3,3,4,128]{3,2,0,1:T(4,128)S(1)} %get-tuple-element.162) | copy-start | bytes 55300
  100.9 9.7 %copy-start.80 = (f32[3,3,4,128]{3,2,0,1:T(4,128)}, f32[3,3,4,128]{3,2,0,1:T(4,128)S(1)}, u32[]{:S(2)}) copy-start(f32[3,3,4,128]{3,2,0,1:T(4,128)S(1)} %get-tuple-element.194) | copy-start | bytes 55300
  102.8 6.9 %copy-start.88 = (f32[3,3,4,128]{3,2,0,1:T(4,128)}, f32[3,3,4,128]{3,2,0,1:T(4,128)S(1)}, u32[]{:S(2)}) copy-start(f32[3,3,4,128]{3,2,0,1:T(4,128)S(1)} %get-tuple-element.190) | copy-start | bytes 55300
  102.8 7.7 %copy-start.86 = (f32[3,3,4,128]{3,2,0,1:T(4,128)}, f32[3,3,4,128]{3,2,0,1:T(4,128)S(1)}, u32[]{:S(2)}) copy-start(f32[3,3,4,128]{3,2,0,1:T(4,128)S(1)} %get-tuple-element.189) | copy-start | bytes 55300
  106.1 9.7 %collective-permute-start.2 = (f32[32,3,2,3,1,128]{5,0,4,3,2,1:T(8,128)S(1)}, f32[32,3,2,3,1,128]{5,0,4,3,2,1:T(8,128)S(1)}, u32[]{:S(2)}, u32[]{:S(2)}) collective-permute-start(f32[32,3,2,3,1,128]{5,0,4,3,2,1:T(8,128)S(1)} %get-tuple-element.115), channel_id=1, source_target_pairs={{0,8},{8,16},{16,24},{24,0},{1,9},{9,17},{17,25},{25,1},{2,10},{10... | collective-permute-start | bytes 884744 | tf_op jit(solution)/shard_map/ppermute | solution.py:15
  106.2 12.9 %collective-permute-start.3 = (f32[32,3,2,3,1,128]{5,0,4,3,2,1:T(8,128)S(1)}, f32[32,3,2,3,1,128]{5,0,4,3,2,1:T(8,128)S(1)}, u32[]{:S(2)}, u32[]{:S(2)}) collective-permute-start(f32[32,3,2,3,1,128]{5,0,4,3,2,1:T(8,128)S(1)} %get-tuple-element.116), channel_id=1, source_target_pairs={{8,0},{16,8},{24,16},{0,24},{9,1},{17,9},{25,17},{1,25},{10,2},{18... | collective-permute-start | bytes 884744 | tf_op jit(solution)/shard_map/ppermute | solution.py:18
  115.9 3.3 copy-start.8
  124.7 8.9 %collective-permute-start.5 = (f32[32,3,2,3,6,1]{0,2,5,4,3,1:T(2,128)}, f32[32,3,2,3,6,1]{0,2,5,4,3,1:T(2,128)}, u32[]{:S(2)}, u32[]{:S(2)}) collective-permute-start(f32[32,3,2,3,6,1]{0,2,5,4,3,1:T(2,128)} %copy.507), channel_id=1, source_target_pairs={{1,0},{2,1},{3,2},{4,3},{5,4},{6,5},{7,6},{0,7},{9,8},{10,9},{11,1... | collective-permute-start | bytes 41480 | tf_op jit(solution)/shard_map/ppermute | solution.py:18
  130.6 10.5 %collective-permute-start.4 = (f32[32,3,2,3,6,1]{0,2,5,4,3,1:T(2,128)}, f32[32,3,2,3,6,1]{0,2,5,4,3,1:T(2,128)}, u32[]{:S(2)}, u32[]{:S(2)}) collective-permute-start(f32[32,3,2,3,6,1]{0,2,5,4,3,1:T(2,128)} %copy.506), channel_id=1, source_target_pairs={{0,1},{1,2},{2,3},{3,4},{4,5},{5,6},{6,7},{7,0},{8,9},{9,10},{10,1... | collective-permute-start | bytes 41480 | tf_op jit(solution)/shard_map/ppermute | solution.py:15
  303.0 134.5 %copy-start.94 = (f32[32,32]{1,0:T(8,128)}, f32[32,32]{1,0:T(8,128)S(1)}, u32[]{:S(2)}) copy-start(f32[32,32]{1,0:T(8,128)S(1)} %get-tuple-element.76) | copy-start | bytes 12292
  305.7 3.9 copy-start.37
  305.7 3.9 copy-start.93
  306.2 4.2 copy-start.2
  306.2 4.2 copy-start.39
  306.2 4.2 copy-start.91
  306.5 8.4 %collective-permute-start.6 = (f32[32,3,2,1,4,128]{5,0,4,3,2,1:T(8,128)S(1)}, f32[32,3,2,1,4,128]{5,0,4,3,2,1:T(8,128)S(1)}, u32[]{:S(2)}, u32[]{:S(2)}) collective-permute-start(f32[32,3,2,1,4,128]{5,0,4,3,2,1:T(8,128)S(1)} %copy.482), channel_id=1, source_target_pairs={{0,32},{32,64},{64,96},{96,128},{128,160},{160,192},{192,224},{224... | collective-permute-start | bytes 1179656 | tf_op jit(solution)/shard_map/ppermute | solution.py:15
  306.5 8.5 %collective-permute-start.7 = (f32[32,3,2,1,4,128]{5,0,4,3,2,1:T(8,128)S(1)}, f32[32,3,2,1,4,128]{5,0,4,3,2,1:T(8,128)S(1)}, u32[]{:S(2)}, u32[]{:S(2)}) collective-permute-start(f32[32,3,2,1,4,128]{5,0,4,3,2,1:T(8,128)S(1)} %copy.482), channel_id=1, source_target_pairs={{32,0},{64,32},{96,64},{128,96},{160,128},{192,160},{224,192},{0,2... | collective-permute-start | bytes 1179656 | tf_op jit(solution)/shard_map/ppermute | solution.py:18
  315.0 2.3 copy-start.85
  315.1 3.0 copy-start.83
  315.1 3.0 copy-start.89
  315.1 3.8 copy-start.81
  315.1 3.8 copy-start.87
  315.2 10.0 %collective-permute-start.8 = (f32[32,3,2,3,1,128]{5,0,4,3,2,1:T(8,128)S(1)}, f32[32,3,2,3,1,128]{5,0,4,3,2,1:T(8,128)S(1)}, u32[]{:S(2)}, u32[]{:S(2)}) collective-permute-start(f32[32,3,2,3,1,128]{5,0,4,3,2,1:T(8,128)S(1)} %get-tuple-element.113), channel_id=1, source_target_pairs={{0,8},{8,16},{16,24},{24,0},{1,9},{9,17},{17,25},{25,1},{2,10},{10... | collective-permute-start | bytes 884744 | tf_op jit(solution)/shard_map/ppermute | solution.py:15
  315.2 15.2 %collective-permute-start.9 = (f32[32,3,2,3,1,128]{5,0,4,3,2,1:T(8,128)S(1)}, f32[32,3,2,3,1,128]{5,0,4,3,2,1:T(8,128)S(1)}, u32[]{:S(2)}, u32[]{:S(2)}) collective-permute-start(f32[32,3,2,3,1,128]{5,0,4,3,2,1:T(8,128)S(1)} %get-tuple-element.114), channel_id=1, source_target_pairs={{8,0},{16,8},{24,16},{0,24},{9,1},{17,9},{25,17},{1,25},{10,2},{18... | collective-permute-start | bytes 884744 | tf_op jit(solution)/shard_map/ppermute | solution.py:18
  325.1 5.3 %copy-start.4 = (f32[32,3,2,3,1,128]{5,0,4,3,2,1:T(8,128)}, f32[32,3,2,3,1,128]{5,0,4,3,2,1:T(8,128)S(1)}, u32[]{:S(2)}) copy-start(f32[32,3,2,3,1,128]{5,0,4,3,2,1:T(8,128)S(1)} %collective-permute-done.8) | copy-start | bytes 884740
  336.0 8.8 %collective-permute-start.11 = (f32[32,3,2,3,6,1]{0,2,5,4,3,1:T(2,128)}, f32[32,3,2,3,6,1]{0,2,5,4,3,1:T(2,128)}, u32[]{:S(2)}, u32[]{:S(2)}) collective-permute-start(f32[32,3,2,3,6,1]{0,2,5,4,3,1:T(2,128)} %copy.509), channel_id=1, source_target_pairs={{1,0},{2,1},{3,2},{4,3},{5,4},{6,5},{7,6},{0,7},{9,8},{10,9},{11,1... | collective-permute-start | bytes 41480 | tf_op jit(solution)/shard_map/ppermute | solution.py:18
  342.8 10.5 %collective-permute-start.10 = (f32[32,3,2,3,6,1]{0,2,5,4,3,1:T(2,128)}, f32[32,3,2,3,6,1]{0,2,5,4,3,1:T(2,128)}, u32[]{:S(2)}, u32[]{:S(2)}) collective-permute-start(f32[32,3,2,3,6,1]{0,2,5,4,3,1:T(2,128)} %copy.508), channel_id=1, source_target_pairs={{0,1},{1,2},{2,3},{3,4},{4,5},{5,6},{6,7},{7,0},{8,9},{9,10},{10,1... | collective-permute-start | bytes 41480 | tf_op jit(solution)/shard_map/ppermute | solution.py:15
  (76 other events, 86.1 us)
where the time goes:
time: 524 us; the launch traced here: 521 us
  blocking collectives  375 us (72%)
  other arithmetic  45.5 us (9%)
  local copies, waits for them, and re-layouts  39 us (7%)
  waiting for transfers between devices  30 us (6%)
  starting transfers between devices  22 us (4%)
  matrix products  7.12 us (1%)
    psum x2, blocking collectives, lanczos_step(): alpha = lax.psum(local_gram(image, basis), ('gx', 'gy', 'gz')) / row_count  150 us
    psum x2, blocking collectives, lanczos_step(): lax.psum(local_gram(residual, residual), ('gx', 'gy', 'gz')) / row_count  146 us
    psum x1, blocking collectives, local(): lax.psum(local_gram(start_block, start_block), ('gx', 'gy', 'gz'))  79.9 us
    ppermute x6, waiting for transfers between devices, extended(): lax.ppermute(lax.slice_in_dim(block, block.shape[dim] - width, None, axis...  21.3 us
    ppermute x6, starting transfers between devices, extended(): lax.ppermute(lax.slice_in_dim(block, 0, width, axis=dim), axis, backward)  18.6 us
    unnamed x203, local copies, waits for them, and re-layouts  17 us
    reduce_sum x42, other arithmetic, apply_hessian(): summed = summed + jnp.sum(coupling[None] * neighbour[:, None], axis=2)  12.5 us
    another operation x9, other arithmetic, inverse_factor(): lower = jnp.linalg.cholesky(gram_matrix)  10.8 us
  transfers between devices with their start and end apart: 12, of which 8 were waited for; matrix products, arithmetic and copies ran while one was open for 6% of the time, Pallas kernels for 0%

commit v1 on v0

v1 whole, which is shorter than its diff:
```python
import functools

import jax
import jax.numpy as jnp
from jax import lax
from jax.experimental import pallas as pl
from jax.experimental.pallas import tpu as pltpu
from jax.sharding import PartitionSpec as P

AXES = ("gx", "gy", "gz")
MESH = pl.DeviceIdType.MESH
HIGHEST = lax.Precision.HIGHEST
F32 = jnp.float32
B = 32
LANES = 128
DIRECTIONS = 14
STEPS = ((1, 0, 0), (0, 1, 0), (1, 1, 0), (0, 0, 1), (1, 0, 1), (0, 1, 1), (1, 1, 1))


def mm(a, b):
    return lax.dot_general(a, b, (((1,), (0,)), ((), ())), precision=HIGHEST, preferred_element_type=F32)


def mt(a, b):
    return lax.dot_general(a, b, (((1,), (1,)), ((), ())), precision=HIGHEST, preferred_element_type=F32)


def factor(gram):
    row_id = lax.broadcasted_iota(jnp.int32, (B, 2 * B), 0)
    lane_id = lax.broadcasted_iota(jnp.int32, (B, 2 * B), 1)
    work = jnp.concatenate([gram, jnp.where(row_id == lane_id, 1.0, 0.0)[:, :B].astype(F32)], axis=1)
    for k in range(B - 1):
        scaled = work[:, k : k + 1] / work[k : k + 1, k : k + 1]
        work = work - jnp.where(row_id > k, scaled * work[k : k + 1, :], 0.0)
    diagonal = jnp.sum(jnp.where(row_id == lane_id, work, 0.0), axis=1, keepdims=True)
    work = work * (1.0 / jnp.sqrt(diagonal))
    upper = jnp.where(row_id <= lane_id, work, 0.0)[:, :B]
    return upper.T, upper, work[:, B:]


def kernel(
    sizes, row_count, offsets,
    start_hbm, pair_hbm, slot_hbm,
    alpha1_ref, alpha2_ref, beta1_ref, beta2_ref, out_ref,
    start, pair, slot, coup, ext_v, ext_w, u_ref, zm1, zm0, zp0, zp1,
    pack_v, pack_w, edge_v, edge_w, gather1, gather2,
    local_sem, hsend_v, hrecv_v, hsend_w, hrecv_w, rsend1, rrecv1, rsend2, rrecv2,
):
    me = [lax.axis_index(axis) for axis in AXES]

    def device(offset):
        return tuple(lax.rem(m + (o % n), n) for m, o, n in zip(me, offset, sizes))

    loads = [
        pltpu.make_async_copy(start_hbm, start, local_sem.at[0]),
        pltpu.make_async_copy(pair_hbm, pair, local_sem.at[1]),
        pltpu.make_async_copy(slot_hbm, slot, local_sem.at[2]),
    ]
    for load in loads:
        load.start()
    barrier = pltpu.get_barrier_semaphore()
    for offset in offsets:
        pl.semaphore_signal(barrier, inc=1, device_id=device(offset), device_id_type=MESH)

    lane = lax.broadcasted_iota(jnp.int32, (B, LANES), 1)

    def halo(ext, pack, edge, send, recv):
        copies = []

        def add(offset, src, dst):
            n = len(copies)
            copies.append(pltpu.make_async_remote_copy(
                src_ref=src, dst_ref=dst, send_sem=send.at[n], recv_sem=recv.at[n],
                device_id=device(offset), device_id_type=MESH))

        for sign in (1, -1):
            far = 0 if sign == 1 else 5
            near = 4 if sign == 1 else 1
            side = 0 if sign == 1 else 2
            sub = 1 if sign == 1 else 0
            add((sign, 0, 0), ext.at[1, pl.ds(1, 4)], ext.at[side, pl.ds(1, 4)])
            add((0, sign, 0), ext.at[1, near], ext.at[1, far])
            add((sign, sign, 0), ext.at[1, near, sub], ext.at[side, far, sub])
            base = 0 if sign == 1 else 4
            src = pack.at[0 if sign == 1 else 1]
            add((0, 0, sign), src, edge.at[base])
            add((sign, 0, sign), src, edge.at[base + 1])
            add((0, sign, sign), src, edge.at[base + 2])
            add((sign, sign, sign), src, edge.at[base + 3])
        return copies

    plane_first = (3, 10, 1, 8, 5, 12)
    plane_last = (0, 7, 2, 9, 4, 11, 6, 13)

    def pack_edges(ext, pack):
        high = jnp.zeros((B, LANES), F32)
        low = jnp.zeros((B, LANES), F32)
        for k in range(24):
            y, rest = divmod(k, 6)
            row = ext[1, 1 + y, rest // 3, rest % 3]
            high = jnp.where(lane == k, pltpu.roll(row, k + 1, 1), high)
            low = jnp.where(lane == k, pltpu.roll(row, k, 1) if k else row, low)
        pack[0] = high
        pack[1] = low

    def down(row, packed, k):
        return jnp.where(lane == 0, pltpu.roll(packed, (LANES - k) % LANES, 1) if k else packed,
                         pltpu.roll(row, 1, 1))

    def up(row, packed, k):
        return jnp.where(lane == LANES - 1, pltpu.roll(packed, LANES - 1 - k, 1),
                         pltpu.roll(row, LANES - 1, 1))

    def shift_plane(ext, edge):
        for c in range(3):
            for y in range(4):
                k = y * 6 + c
                zm1[1, y + 1, c] = down(ext[1, 1 + y, 1, c], edge[0], k + 3)
                zm0[y, c] = down(ext[1, 1 + y, 0, c], edge[0], k)
                zp0[0, y, c] = up(ext[1, 1 + y, 0, c], edge[4], k)
                zp1[y, c] = up(ext[1, 1 + y, 1, c], edge[4], k + 3)
            zm1[1, 0, c] = down(ext[1, 0, 1, c], edge[2], 21 + c)
            zp0[0, 4, c] = up(ext[1, 5, 0, c], edge[6], c)

    def shift_sides(ext, edge):
        for c in range(3):
            for y in range(4):
                k = y * 6 + c
                zm1[0, y + 1, c] = down(ext[0, 1 + y, 1, c], edge[1], k + 3)
                zp0[1, y, c] = up(ext[2, 1 + y, 0, c], edge[5], k)
            zm1[0, 0, c] = down(ext[0, 0, 1, c], edge[3], 21 + c)
            zp0[1, 4, c] = up(ext[2, 5, 0, c], edge[7], c)

    def plane_terms(ext, sub, y):
        terms = []
        for b1 in range(2):
            if sub == 0:
                terms.append((b1 * 2, ext, (1, 1 + y - b1, 1)))
                terms.append((b1 * 2 + 1, zm1, (1, y - b1 + 1)))
            else:
                terms.append((b1 * 2, ext, (1, 1 + y + b1, 0)))
                terms.append((b1 * 2 + 1, zp0, (0, y + b1)))
        terms.append((10, ext, (1, 2 + y, sub)))
        terms.append((11, ext, (1, y, sub)))
        if sub == 0:
            terms.append((12, zp0, (0, y)))
            terms.append((13, zm0, (y,)))
        else:
            terms.append((12, zp1, (y,)))
            terms.append((13, zm1, (1, y + 1)))
        terms.append((14, ext, (1, 1 + y, sub)))
        return terms

    def side_terms(ext, sub, y):
        terms = []
        for b1 in range(2):
            if sub == 0:
                terms.append((4 + b1 * 2, ext, (0, 1 + y - b1, 1)))
                terms.append((5 + b1 * 2, zm1, (0, y - b1 + 1)))
            else:
                terms.append((4 + b1 * 2, ext, (2, 1 + y + b1, 0)))
                terms.append((5 + b1 * 2, zp0, (1, y + b1)))
        terms.append((8, ext, (2, 1 + y, sub)))
        terms.append((9, ext, (0, 1 + y, sub)))
        return terms

    def apply_terms(terms_of, ext, write, read):
        def body(y, carry):
            for sub in range(2):
                total = [read(y, sub, i) if read else jnp.zeros((B, LANES), F32) for i in range(3)]
                for o, ref, index in terms_of(ext, sub, y):
                    for j in range(3):
                        row = ref[index + (j,)]
                        for i in range(3):
                            block = coup[o, i * 3 + j, pl.ds(sub * 4 + y, 1), :]
                            total[i] = total[i] + block * row
                for i in range(3):
                    write(y, sub, i, total[i])
            return carry

        lax.fori_loop(0, 4, body, 0)

    def wide(rows_of, y):
        return jnp.concatenate([rows_of(y, sc // 3, sc % 3) for sc in range(6)], axis=1)

    def v_row(y, s, c):
        return ext_v[1, 1 + y, s, c]

    def w_row(y, s, c):
        return ext_w[1, 1 + y, s, c]

    def u_row(y, s, c):
        return u_ref[y, s, c]

    def write_w(y, s, c, value):
        ext_w[1, 1 + y, s, c] = value

    def write_u(y, s, c, value):
        u_ref[y, s, c] = value

    def gram(lefts, rights):
        def body(y, carry):
            right = jnp.concatenate([wide(rows, y) for rows in rights], axis=0)
            left = jnp.concatenate([wide(rows, y) for rows in lefts], axis=0)
            return carry + mt(left, right)

        return lax.fori_loop(0, 4, body, jnp.zeros((B * len(lefts), B * len(rights)), F32))

    base = [0, sizes[0], sizes[0] + sizes[1]]
    sem_base = [0, sizes[0] - 1, sizes[0] + sizes[1] - 2]

    def reduce_start(axis, gather, send, recv):
        copies = []
        for d in range(1, sizes[axis]):
            offset = tuple(d if a == axis else 0 for a in range(3))
            n = sem_base[axis] + d - 1
            copy = pltpu.make_async_remote_copy(
                src_ref=gather.at[base[axis]], dst_ref=gather.at[base[axis] + d],
                send_sem=send.at[n], recv_sem=recv.at[n], device_id=device(offset), device_id_type=MESH)
            copy.start()
            copies.append(copy)
        return copies

    def reduce_finish(axis, gather, copies):
        for copy in copies:
            copy.wait_recv()
        size = sizes[axis]
        total = None
        for m in range(size):
            term = gather[base[axis] + lax.rem(me[axis] + size - m, size)]
            total = term if total is None else total + term
        return total

    loads[0].wait()
    for y in range(4):
        for s in range(2):
            for c in range(3):
                ext_v[1, 1 + y, s, c] = start[pl.ds(c * 8 + s * 4 + y, B, stride=24), :]
    pack_edges(ext_v, pack_v)
    pl.semaphore_wait(barrier, len(offsets))
    halo_v = halo(ext_v, pack_v, edge_v, hsend_v, hrecv_v)
    for n in (0, 7, 1, 8, 2, 9, 3, 10, 4, 11, 5, 12, 6, 13):
        halo_v[n].start()

    loads[1].wait()
    loads[2].wait()

    def select(o, carry):
        chosen = [slot[k] == o for k in range(16)]
        result = []
        for e in range(9):
            value = jnp.zeros((8, LANES), F32)
            for k in range(16):
                value = jnp.where(chosen[k], pair[e, k], value)
            coup[o, e] = value
            result.append(carry[e] + value)
        return tuple(result)

    sums = lax.fori_loop(0, DIRECTIONS, select, tuple(jnp.zeros((8, LANES), F32) for _ in range(9)))
    for i in range(3):
        for j in range(3):
            coup[DIRECTIONS, i * 3 + j] = -0.5 * (sums[i * 3 + j] + sums[j * 3 + i])

    moment0 = gram([v_row], [v_row])

    for n in plane_first:
        halo_v[n].wait_recv()
    shift_plane(ext_v, edge_v)
    apply_terms(plane_terms, ext_v, write_w, None)
    for n in plane_last:
        halo_v[n].wait_recv()
    shift_sides(ext_v, edge_v)
    apply_terms(side_terms, ext_v, write_w, w_row)

    pack_edges(ext_w, pack_w)
    halo_w = halo(ext_w, pack_w, edge_w, hsend_w, hrecv_w)
    for n in (0, 7, 1, 8, 2, 9, 3, 10, 4, 11, 5, 12, 6, 13):
        halo_w[n].start()

    pad = jnp.zeros((B, B), F32)
    gather1[base[0]] = jnp.concatenate([moment0, gram([w_row], [v_row, w_row]), pad], axis=1)
    sum1 = [reduce_start(0, gather1, rsend1, rrecv1)]

    for n in plane_first:
        halo_w[n].wait_recv()
    shift_plane(ext_w, edge_w)
    apply_terms(plane_terms, ext_w, write_u, None)
    gather1[base[1]] = reduce_finish(0, gather1, sum1[0])
    sum1.append(reduce_start(1, gather1, rsend1, rrecv1))
    for n in plane_last:
        halo_w[n].wait_recv()
    shift_sides(ext_w, edge_w)
    apply_terms(side_terms, ext_w, write_u, u_row)
    gather1[base[2]] = reduce_finish(1, gather1, sum1[1])
    sum1.append(reduce_start(2, gather1, rsend1, rrecv1))

    gather2[base[0]] = jnp.concatenate([gram([u_row], [w_row, u_row]), pad, pad], axis=1)
    sum2 = [reduce_start(0, gather2, rsend2, rrecv2)]

    first = reduce_finish(2, gather1, sum1[2]) * (1.0 / row_count)
    m0, m1, m2 = first[:, :B], first[:, B : 2 * B], first[:, 2 * B : 3 * B]
    _, _, inverse0 = factor(m0)

    gather2[base[1]] = reduce_finish(0, gather2, sum2[0])
    sum2.append(reduce_start(1, gather2, rsend2, rrecv2))

    alpha1 = mt(mm(inverse0, m1), inverse0)
    square1 = mt(mm(inverse0, m2), inverse0)
    beta1, upper1, inverse1 = factor(square1 - mt(alpha1, alpha1))

    gather2[base[2]] = reduce_finish(1, gather2, sum2[1])
    sum2.append(reduce_start(2, gather2, rsend2, rrecv2))

    on_w = mm(inverse1, inverse0)
    on_v = -mm(mm(inverse1, alpha1), inverse0)
    on_m2 = mm(on_v, m2)
    known_alpha = mt(on_m2, on_w) + mt(on_w, on_m2) + mt(mm(on_v, m1), on_v)
    known_square = mt(on_m2, on_v) - mt(upper1, upper1)
    from_v = mm(upper1, inverse0)

    second = reduce_finish(2, gather2, sum2[2]) * (1.0 / row_count)
    m3, m4 = second[:, :B], second[:, B : 2 * B]
    on_m3 = mm(on_w, m3)
    alpha2 = mt(on_m3, on_w) + known_alpha
    square2 = (mt(mm(on_w, m4), on_w) + mt(on_m3, on_v)) + (mt(on_v, on_m3) + known_square)
    beta2, _, inverse2 = factor(square2 - mt(alpha2, alpha2))

    weights = jnp.concatenate(
        [-(mm(alpha2, on_v) + from_v), on_v - mm(alpha2, on_w), on_w], axis=1)
    weights = mm(inverse2, weights)

    for y in range(4):
        for s in range(2):
            for c in range(3):
                rows = jnp.concatenate([v_row(y, s, c), w_row(y, s, c), u_row(y, s, c)], axis=0)
                out_ref[pl.ds(c * 8 + s * 4 + y, B, stride=24), :] = mm(weights, rows)

    alpha1_ref[...] = alpha1
    alpha2_ref[...] = alpha2
    beta1_ref[...] = beta1
    beta2_ref[...] = beta2
    for copy in halo_v + halo_w + sum1[0] + sum1[1] + sum1[2] + sum2[0] + sum2[1] + sum2[2]:
        copy.wait_send()


def local(sizes, start_block, pair_blocks, slot_map):
    devices = sizes[0] * sizes[1] * sizes[2]
    row_count = start_block[0].size * devices
    offsets = set()
    for step in STEPS:
        for sign in (1, -1):
            offsets.add(tuple((sign * a) % n for a, n in zip(step, sizes)))
    for axis in range(3):
        for d in range(1, sizes[axis]):
            offsets.add(tuple(d if a == axis else 0 for a in range(3)))
    offsets = sorted(offsets)
    slots = sum(sizes)
    links = slots - 3
    dma = pltpu.SemaphoreType.DMA
    small = jax.ShapeDtypeStruct((B, B), F32)
    vmem = pl.BlockSpec(memory_space=pltpu.VMEM)
    anywhere = pl.BlockSpec(memory_space=pl.ANY)
    extended = pltpu.VMEM((3, 6, 2, 3, B, LANES), F32)
    results = pl.pallas_call(
        functools.partial(kernel, sizes, row_count, offsets),
        out_shape=(small, small, small, small, jax.ShapeDtypeStruct((B * 24, LANES), F32)),
        in_specs=[anywhere] * 3,
        out_specs=(vmem,) * 5,
        scratch_shapes=[
            pltpu.VMEM((B * 24, LANES), F32),
            pltpu.VMEM((9, 16, 8, LANES), F32),
            pltpu.VMEM((16, 8, LANES), jnp.int32),
            pltpu.VMEM((DIRECTIONS + 1, 9, 8, LANES), F32),
            extended,
            extended,
            pltpu.VMEM((4, 2, 3, B, LANES), F32),
            pltpu.VMEM((2, 5, 3, B, LANES), F32),
            pltpu.VMEM((4, 3, B, LANES), F32),
            pltpu.VMEM((2, 5, 3, B, LANES), F32),
            pltpu.VMEM((4, 3, B, LANES), F32),
            pltpu.VMEM((2, B, LANES), F32),
            pltpu.VMEM((2, B, LANES), F32),
            pltpu.VMEM((8, B, LANES), F32),
            pltpu.VMEM((8, B, LANES), F32),
            pltpu.VMEM((slots, B, LANES), F32),
            pltpu.VMEM((slots, B, LANES), F32),
            dma((3,)),
            dma((14,)), dma((14,)), dma((14,)), dma((14,)),
            dma((links,)), dma((links,)), dma((links,)), dma((links,)),
        ],
        compiler_params=pltpu.CompilerParams(
            collective_id=0, has_side_effects=True, vmem_limit_bytes=32 * 1024 * 1024),
        name="lanczos",
    )(
        start_block.reshape(B * 24, LANES),
        pair_blocks.reshape(9, 16, 8, LANES),
        slot_map.reshape(16, 8, LANES),
    )
    alpha1, alpha2, beta1, beta2, basis3 = results
    return alpha1, alpha2, beta1, beta2, basis3.reshape(start_block.shape)


def solution(mesh):
    sizes = tuple(mesh.shape[axis] for axis in AXES)
    in_specs = (
        P(None, None, None, "gx", "gy", "gz"),
        P(None, None, None, None, "gx", "gy", "gz"),
        P(None, None, "gx", "gy", "gz"),
    )
    out_specs = (P(), P(), P(), P(), P(None, None, None, "gx", "gy", "gz"))
    return jax.shard_map(
        functools.partial(local, sizes), mesh=mesh, in_specs=in_specs, out_specs=out_specs, check_vma=False)
```

time: 524 us -> 82.3 us (0.16)
  blocking collectives: 375 us -> 0 us
  Pallas kernels: 0 us -> 75.1 us
  other arithmetic: 45.5 us -> 0 us
  local copies, waits for them, and re-layouts: 39 us -> 6.06 us
  waiting for transfers between devices: 30 us -> 0 us
  starting transfers between devices: 22 us -> 0 us
  matrix products: 7.12 us -> 0 us
    psum x5 -> x0, blocking collectives: 375 us -> none  [the longest x2 150 us: lanczos_step(): alpha = lax.psum(local_gram(image, basis), ('gx', 'gy', 'gz')) / row_count]
    pallas_call x0 -> x1, Pallas kernels: none -> 75.1 us  [local(): pl.pallas_call(functools.partial(kernel, sizes, row_count, offsets), out_...]
    ppermute x12 -> x0, waiting for transfers between devices: 30 us -> none  [the longest x6 21.3 us: extended(): lax.ppermute(lax.slice_in_dim(block, block.shape[dim] - width, None, axis...]
    ppermute x12 -> x0, starting transfers between devices: 22 us -> none  [the longest x6 18.6 us: extended(): lax.ppermute(lax.slice_in_dim(block, 0, width, axis=dim), axis, backward)]
    another operation x17 -> x0, other arithmetic: 20.8 us -> none  [the longest x9 10.8 us: inverse_factor(): lower = jnp.linalg.cholesky(gram_matrix)]
    reduce_sum x45 -> x0, other arithmetic: 16.6 us -> none  [the longest x42 12.5 us: apply_hessian(): summed = summed + jnp.sum(coupling[None] * neighbour[:, None], axis=2)]
    unnamed x203 -> x11, local copies, waits for them, and re-layouts: 17 us -> 6.06 us
    ppermute x4 -> x0, local copies, waits for them, and re-layouts: 7.29 us -> none  [the longest x2 4.25 us: extended(): lax.ppermute(lax.slice_in_dim(block, 0, width, axis=dim), axis, backward)]
  transfers between devices with their start and end apart: 12 -> 0, of which waited for: 8 -> 0; matrix products, arithmetic and copies ran while one was open for 6% -> 0% of each run, Pallas kernels for 0% -> 0%
where the time goes in v1:
time: 82.3 us; the launch traced here: 81.8 us
  Pallas kernels  75.1 us (91%)
  local copies, waits for them, and re-layouts  6.06 us (7%)
    pallas_call x1, Pallas kernels, local(): pl.pallas_call(functools.partial(kernel, sizes, row_count, offsets), out_...  75.1 us
    unnamed x11, local copies, waits for them, and re-layouts  6.06 us

profile of v1, /device:TPU:32, one launch (start us, length us, event | category | flops | bytes accessed | tf_op | source)
XLA Modules:
  0.0 81.8 jit_solution(1933667374887235527)
XLA Ops:
  0.6 0.0 copy-start
  0.6 1.1 %copy-done = f32[3,3,16,2,1,4,128]{6,5,4,3,2,1,0:T(4,128)S(1)} copy-done((f32[3,3,16,2,1,4,128]{6,5,4,3,2,1,0:T(4,128)S(1)}, f32[3,3,16,2,1,4,128]{6,5,4,3,2,1,0:T(4,128)}, u32[]{:S(2)}) %copy-start) | copy-done | bytes 589848
  1.7 0.0 copy-start.1
  1.7 1.0 %copy-done.1 = f32[32,3,2,1,4,128]{5,4,3,2,1,0:T(4,128)S(1)} copy-done((f32[32,3,2,1,4,128]{5,4,3,2,1,0:T(4,128)S(1)}, f32[32,3,2,1,4,128]{5,4,3,2,1,0:T(4,128)}, u32[]{:S(2)}) %copy-start.1) | copy-done | bytes 393240
  2.7 0.0 copy-start.2
  2.7 0.8 %copy-done.2 = s32[16,2,1,4,128]{4,3,2,1,0:T(4,128)S(1)} copy-done((s32[16,2,1,4,128]{4,3,2,1,0:T(4,128)S(1)}, s32[16,2,1,4,128]{4,3,2,1,0:T(4,128)}, u32[]{:S(2)}) %copy-start.2) | copy-done | bytes 65560
  3.5 75.1 %lanczos.1 = (f32[32,32]{1,0:T(8,128)S(1)}, f32[32,32]{1,0:T(8,128)S(1)}, f32[32,32]{1,0:T(8,128)S(1)}, f32[32,32]{1,0:T(8,128)S(1)}, f32[768,128]{1,0:T(8,128)S(1)}) custom-call(f32[768,128]{1,0:T(8,128)S(1)} %bitcast.8, f32[9,16,8,128]{3,2,1,0:T(8,128)S(1)} %bitcast.6, s32[16,8,128]{2,1,0:T(8,128)S(1)} %bitcast.9), custom_call_target="tpu_custom_call" | custom-call | tf_op jit(solution)/shard_map/lanczos/pallas_call | solution.py:364
  78.6 0.6 copy.14
  79.2 0.6 copy.15
  79.9 0.6 copy.16
  80.5 0.6 copy.17
  81.1 0.7 copy.18
Async XLA Ops:
  0.6 1.1 %copy-start = (f32[3,3,16,2,1,4,128]{6,5,4,3,2,1,0:T(4,128)S(1)}, f32[3,3,16,2,1,4,128]{6,5,4,3,2,1,0:T(4,128)}, u32[]{:S(2)}) copy-start(f32[3,3,16,2,1,4,128]{6,5,4,3,2,1,0:T(4,128)} %param.4) | copy-start | bytes 1769476
  1.7 1.0 %copy-start.1 = (f32[32,3,2,1,4,128]{5,4,3,2,1,0:T(4,128)S(1)}, f32[32,3,2,1,4,128]{5,4,3,2,1,0:T(4,128)}, u32[]{:S(2)}) copy-start(f32[32,3,2,1,4,128]{5,4,3,2,1,0:T(4,128)} %param.3) | copy-start | bytes 1179652
  2.7 0.8 %copy-start.2 = (s32[16,2,1,4,128]{4,3,2,1,0:T(4,128)S(1)}, s32[16,2,1,4,128]{4,3,2,1,0:T(4,128)}, u32[]{:S(2)}) copy-start(s32[16,2,1,4,128]{4,3,2,1,0:T(4,128)} %param.5) | copy-start | bytes 196612

commit v2 on v1

--- a/solution.py
+++ b/solution.py
@@ -1,4 +1,5 @@
 import functools
+import itertools
 
 import jax
 import jax.numpy as jnp
@@ -14,6 +15,7 @@
 B = 32
 LANES = 128
 DIRECTIONS = 14
+DIGITS = {"core": 2, "x": 4, "y": 4, "z_lo": 4, "z_hi": 2}
 STEPS = ((1, 0, 0), (0, 1, 0), (1, 1, 0), (0, 0, 1), (1, 0, 1), (0, 1, 1), (1, 1, 1))
 
 
@@ -39,7 +41,7 @@
 
 
 def kernel(
-    sizes, row_count, offsets,
+    sizes, row_count, offsets, stages, moves,
     start_hbm, pair_hbm, slot_hbm,
     alpha1_ref, alpha2_ref, beta1_ref, beta2_ref, out_ref,
     start, pair, slot, coup, ext_v, ext_w, u_ref, zm1, zm0, zp0, zp1,
@@ -50,6 +52,15 @@
 
     def device(offset):
         return tuple(lax.rem(m + (o % n), n) for m, o, n in zip(me, offset, sizes))
+
+    place = {"core": lax.rem(me[0], 2), "x": me[0] // 2, "y": me[2] // 2, "z_lo": me[1], "z_hi": lax.rem(me[2], 2)}
+
+    def partner(stage, move):
+        there = dict(place)
+        for digit, step in zip(stages[stage]["digits"], move):
+            if step:
+                there[digit] = lax.rem(place[digit] + step, DIGITS[digit])
+        return (2 * there["x"] + there["core"], there["z_lo"], 2 * there["y"] + there["z_hi"])
 
     loads = [
         pltpu.make_async_copy(start_hbm, start, local_sem.at[0]),
@@ -61,8 +72,11 @@
     barrier = pltpu.get_barrier_semaphore()
     for offset in offsets:
         pl.semaphore_signal(barrier, inc=1, device_id=device(offset), device_id_type=MESH)
-
-    lane = lax.broadcasted_iota(jnp.int32, (B, LANES), 1)
+    for stage, move in moves:
+        pl.semaphore_signal(barrier, inc=1, device_id=partner(stage, move), device_id_type=MESH)
+
+    lane = lax.broadcasted_iota(jnp.int32, (8, LANES), 1)
+    tiles = [pl.ds(8 * q, 8) for q in range(B // 8)]
 
     def halo(ext, pack, edge, send, recv):
         copies = []
@@ -92,44 +106,52 @@
     plane_first = (3, 10, 1, 8, 5, 12)
     plane_last = (0, 7, 2, 9, 4, 11, 6, 13)
 
+    def turn(tile, amount):
+        amount = amount % LANES
+        return pltpu.roll(tile, amount, 1) if amount else tile
+
     def pack_edges(ext, pack):
-        high = jnp.zeros((B, LANES), F32)
-        low = jnp.zeros((B, LANES), F32)
+        high = jnp.zeros((8, LANES), F32)
+        low = jnp.zeros((8, LANES), F32)
         for k in range(24):
             y, rest = divmod(k, 6)
-            row = ext[1, 1 + y, rest // 3, rest % 3]
-            high = jnp.where(lane == k, pltpu.roll(row, k + 1, 1), high)
-            low = jnp.where(lane == k, pltpu.roll(row, k, 1) if k else row, low)
+            for q, tile in enumerate(tiles):
+                row = ext[1, 1 + y, rest // 3, rest % 3, tile]
+                here = lane == 32 * q + k
+                high = jnp.where(here, turn(row, 32 * q + k + 1), high)
+                low = jnp.where(here, turn(row, 32 * q + k), low)
         pack[0] = high
         pack[1] = low
 
-    def down(row, packed, k):
-        return jnp.where(lane == 0, pltpu.roll(packed, (LANES - k) % LANES, 1) if k else packed,
-                         pltpu.roll(row, 1, 1))
-
-    def up(row, packed, k):
-        return jnp.where(lane == LANES - 1, pltpu.roll(packed, LANES - 1 - k, 1),
-                         pltpu.roll(row, LANES - 1, 1))
+    def down(dst, dst_index, src, src_index, packed, k):
+        for q, tile in enumerate(tiles):
+            dst[dst_index + (tile,)] = jnp.where(
+                lane == 0, turn(packed, -(32 * q + k)), turn(src[src_index + (tile,)], 1))
+
+    def up(dst, dst_index, src, src_index, packed, k):
+        for q, tile in enumerate(tiles):
+            dst[dst_index + (tile,)] = jnp.where(
+                lane == LANES - 1, turn(packed, LANES - 1 - (32 * q + k)), turn(src[src_index + (tile,)], -1))
 
     def shift_plane(ext, edge):
         for c in range(3):
             for y in range(4):
                 k = y * 6 + c
-                zm1[1, y + 1, c] = down(ext[1, 1 + y, 1, c], edge[0], k + 3)
-                zm0[y, c] = down(ext[1, 1 + y, 0, c], edge[0], k)
-                zp0[0, y, c] = up(ext[1, 1 + y, 0, c], edge[4], k)
-                zp1[y, c] = up(ext[1, 1 + y, 1, c], edge[4], k + 3)
-            zm1[1, 0, c] = down(ext[1, 0, 1, c], edge[2], 21 + c)
-            zp0[0, 4, c] = up(ext[1, 5, 0, c], edge[6], c)
+                down(zm1, (1, y + 1, c), ext, (1, 1 + y, 1, c), edge[0], k + 3)
+                down(zm0, (y, c), ext, (1, 1 + y, 0, c), edge[0], k)
+                up(zp0, (0, y, c), ext, (1, 1 + y, 0, c), edge[4], k)
+                up(zp1, (y, c), ext, (1, 1 + y, 1, c), edge[4], k + 3)
+            down(zm1, (1, 0, c), ext, (1, 0, 1, c), edge[2], 21 + c)
+            up(zp0, (0, 4, c), ext, (1, 5, 0, c), edge[6], c)
 
     def shift_sides(ext, edge):
         for c in range(3):
             for y in range(4):
                 k = y * 6 + c
-                zm1[0, y + 1, c] = down(ext[0, 1 + y, 1, c], edge[1], k + 3)
-                zp0[1, y, c] = up(ext[2, 1 + y, 0, c], edge[5], k)
-            zm1[0, 0, c] = down(ext[0, 0, 1, c], edge[3], 21 + c)
-            zp0[1, 4, c] = up(ext[2, 5, 0, c], edge[7], c)
+                down(zm1, (0, y + 1, c), ext, (0, 1 + y, 1, c), edge[1], k + 3)
+                up(zp0, (1, y, c), ext, (2, 1 + y, 0, c), edge[5], k)
+            down(zm1, (0, 0, c), ext, (0, 0, 1, c), edge[3], 21 + c)
+            up(zp0, (1, 4, c), ext, (2, 5, 0, c), edge[7], c)
 
     def plane_terms(ext, sub, y):
         terms = []
@@ -206,30 +228,38 @@
 
         return lax.fori_loop(0, 4, body, jnp.zeros((B * len(lefts), B * len(rights)), F32))
 
-    base = [0, sizes[0], sizes[0] + sizes[1]]
-    sem_base = [0, sizes[0] - 1, sizes[0] + sizes[1] - 2]
-
-    def reduce_start(axis, gather, send, recv):
+    def reduce_start(stage, gather, value, send, recv):
+        first, count = stages[stage]["slot"], len(stages[stage]["moves"])
+        gather[first] = value
         copies = []
-        for d in range(1, sizes[axis]):
-            offset = tuple(d if a == axis else 0 for a in range(3))
-            n = sem_base[axis] + d - 1
+        for n in range(1, count):
             copy = pltpu.make_async_remote_copy(
-                src_ref=gather.at[base[axis]], dst_ref=gather.at[base[axis] + d],
-                send_sem=send.at[n], recv_sem=recv.at[n], device_id=device(offset), device_id_type=MESH)
+                src_ref=gather.at[first], dst_ref=gather.at[first + n],
+                send_sem=send.at[first + n], recv_sem=recv.at[first + n],
+                device_id=partner(stage, stages[stage]["moves"][n]), device_id_type=MESH)
             copy.start()
             copies.append(copy)
         return copies
 
-    def reduce_finish(axis, gather, copies):
+    def reduce_finish(stage, gather, copies):
         for copy in copies:
             copy.wait_recv()
-        size = sizes[axis]
+        first = stages[stage]["slot"]
         total = None
-        for m in range(size):
-            term = gather[base[axis] + lax.rem(me[axis] + size - m, size)]
+        for move in stages[stage]["moves"]:
+            slot = first
+            for digit, step in zip(stages[stage]["digits"], move):
+                slot = slot + lax.rem(place[digit] + DIGITS[digit] - step, DIGITS[digit]) * stages[stage]["stride"][digit]
+            term = gather[slot]
             total = term if total is None else total + term
         return total
+
+    def packed(matrices):
+        return jnp.concatenate(
+            [jnp.concatenate([m[8 * q : 8 * q + 8] for q in range(4)], axis=1) for m in matrices], axis=0)
+
+    def unpacked(tile):
+        return jnp.concatenate([tile[:, B * q : B * q + B] for q in range(4)], axis=0)
 
     loads[0].wait()
     for y in range(4):
@@ -237,9 +267,9 @@
             for c in range(3):
                 ext_v[1, 1 + y, s, c] = start[pl.ds(c * 8 + s * 4 + y, B, stride=24), :]
     pack_edges(ext_v, pack_v)
-    pl.semaphore_wait(barrier, len(offsets))
+    pl.semaphore_wait(barrier, len(offsets) + len(moves))
     halo_v = halo(ext_v, pack_v, edge_v, hsend_v, hrecv_v)
-    for n in (0, 7, 1, 8, 2, 9, 3, 10, 4, 11, 5, 12, 6, 13):
+    for n in (3, 10, 5, 12, 4, 11, 6, 13, 1, 8, 0, 7, 2, 9):
         halo_v[n].start()
 
     loads[1].wait()
@@ -274,42 +304,40 @@
 
     pack_edges(ext_w, pack_w)
     halo_w = halo(ext_w, pack_w, edge_w, hsend_w, hrecv_w)
-    for n in (0, 7, 1, 8, 2, 9, 3, 10, 4, 11, 5, 12, 6, 13):
+    for n in (3, 10, 5, 12, 4, 11, 6, 13, 1, 8, 0, 7, 2, 9):
         halo_w[n].start()
 
-    pad = jnp.zeros((B, B), F32)
-    gather1[base[0]] = jnp.concatenate([moment0, gram([w_row], [v_row, w_row]), pad], axis=1)
-    sum1 = [reduce_start(0, gather1, rsend1, rrecv1)]
+    moments = gram([w_row], [v_row, w_row])
+    sum1 = [reduce_start(0, gather1, packed([moment0, moments[:, :B], moments[:, B:]]), rsend1, rrecv1)]
 
     for n in plane_first:
         halo_w[n].wait_recv()
     shift_plane(ext_w, edge_w)
+    total = reduce_finish(0, gather1, sum1[0])
+    sum1.append(reduce_start(1, gather1, total, rsend1, rrecv1))
     apply_terms(plane_terms, ext_w, write_u, None)
-    gather1[base[1]] = reduce_finish(0, gather1, sum1[0])
-    sum1.append(reduce_start(1, gather1, rsend1, rrecv1))
+    total = reduce_finish(1, gather1, sum1[1])
+    sum1.append(reduce_start(2, gather1, total, rsend1, rrecv1))
     for n in plane_last:
         halo_w[n].wait_recv()
     shift_sides(ext_w, edge_w)
     apply_terms(side_terms, ext_w, write_u, u_row)
-    gather1[base[2]] = reduce_finish(1, gather1, sum1[1])
-    sum1.append(reduce_start(2, gather1, rsend1, rrecv1))
-
-    gather2[base[0]] = jnp.concatenate([gram([u_row], [w_row, u_row]), pad, pad], axis=1)
-    sum2 = [reduce_start(0, gather2, rsend2, rrecv2)]
-
+
+    moments = gram([u_row], [w_row, u_row])
+    sum2 = [reduce_start(0, gather2, packed([moments[:, :B], moments[:, B:]]), rsend2, rrecv2)]
     first = reduce_finish(2, gather1, sum1[2]) * (1.0 / row_count)
-    m0, m1, m2 = first[:, :B], first[:, B : 2 * B], first[:, 2 * B : 3 * B]
+    m0, m1, m2 = unpacked(first[:8]), unpacked(first[8:16]), unpacked(first[16:])
+    total = reduce_finish(0, gather2, sum2[0])
+    sum2.append(reduce_start(1, gather2, total, rsend2, rrecv2))
+
     _, _, inverse0 = factor(m0)
-
-    gather2[base[1]] = reduce_finish(0, gather2, sum2[0])
-    sum2.append(reduce_start(1, gather2, rsend2, rrecv2))
 
     alpha1 = mt(mm(inverse0, m1), inverse0)
     square1 = mt(mm(inverse0, m2), inverse0)
+    total = reduce_finish(1, gather2, sum2[1])
+    sum2.append(reduce_start(2, gather2, total, rsend2, rrecv2))
+
     beta1, upper1, inverse1 = factor(square1 - mt(alpha1, alpha1))
-
-    gather2[base[2]] = reduce_finish(1, gather2, sum2[1])
-    sum2.append(reduce_start(2, gather2, rsend2, rrecv2))
 
     on_w = mm(inverse1, inverse0)
     on_v = -mm(mm(inverse1, alpha1), inverse0)
@@ -319,7 +347,7 @@
     from_v = mm(upper1, inverse0)
 
     second = reduce_finish(2, gather2, sum2[2]) * (1.0 / row_count)
-    m3, m4 = second[:, :B], second[:, B : 2 * B]
+    m3, m4 = unpacked(second[:8]), unpacked(second[8:])
     on_m3 = mm(on_w, m3)
     alpha2 = mt(on_m3, on_w) + known_alpha
     square2 = (mt(mm(on_w, m4), on_w) + mt(on_m3, on_v)) + (mt(on_v, on_m3) + known_square)
@@ -343,28 +371,44 @@
         copy.wait_send()
 
 
+def deliver(*refs):
+    sem = refs[10]
+    copies = [pltpu.make_async_copy(refs[n], refs[5 + n], sem.at[n]) for n in range(5)]
+    for copy in copies:
+        copy.start()
+    for copy in copies:
+        copy.wait()
+
+
 def local(sizes, start_block, pair_blocks, slot_map):
     devices = sizes[0] * sizes[1] * sizes[2]
     row_count = start_block[0].size * devices
+    if sizes != (2 * DIGITS["x"], DIGITS["z_lo"], 2 * DIGITS["y"]):
+        raise ValueError("unexpected mesh")
     offsets = set()
     for step in STEPS:
         for sign in (1, -1):
             offsets.add(tuple((sign * a) % n for a, n in zip(step, sizes)))
-    for axis in range(3):
-        for d in range(1, sizes[axis]):
-            offsets.add(tuple(d if a == axis else 0 for a in range(3)))
     offsets = sorted(offsets)
-    slots = sum(sizes)
-    links = slots - 3
+    stages, moves, slots = [], [], 0
+    for digits in (("core",), ("x", "y"), ("z_lo", "z_hi")):
+        steps = list(itertools.product(*[range(DIGITS[digit]) for digit in digits]))
+        stride, span = {}, 1
+        for digit in reversed(digits):
+            stride[digit] = span
+            span *= DIGITS[digit]
+        stages.append({"digits": digits, "moves": steps, "stride": stride, "slot": slots})
+        slots += len(steps)
+        moves += [(len(stages) - 1, step) for step in steps[1:]]
     dma = pltpu.SemaphoreType.DMA
     small = jax.ShapeDtypeStruct((B, B), F32)
     vmem = pl.BlockSpec(memory_space=pltpu.VMEM)
-    anywhere = pl.BlockSpec(memory_space=pl.ANY)
+    hbm = pl.BlockSpec(memory_space=pltpu.HBM)
     extended = pltpu.VMEM((3, 6, 2, 3, B, LANES), F32)
     results = pl.pallas_call(
-        functools.partial(kernel, sizes, row_count, offsets),
+        functools.partial(kernel, sizes, row_count, offsets, stages, moves),
         out_shape=(small, small, small, small, jax.ShapeDtypeStruct((B * 24, LANES), F32)),
-        in_specs=[anywhere] * 3,
+        in_specs=[hbm] * 3,
         out_specs=(vmem,) * 5,
         scratch_shapes=[
             pltpu.VMEM((B * 24, LANES), F32),
@@ -378,25 +422,33 @@
             pltpu.VMEM((4, 3, B, LANES), F32),
             pltpu.VMEM((2, 5, 3, B, LANES), F32),
             pltpu.VMEM((4, 3, B, LANES), F32),
-            pltpu.VMEM((2, B, LANES), F32),
-            pltpu.VMEM((2, B, LANES), F32),
-            pltpu.VMEM((8, B, LANES), F32),
-            pltpu.VMEM((8, B, LANES), F32),
-            pltpu.VMEM((slots, B, LANES), F32),
-            pltpu.VMEM((slots, B, LANES), F32),
+            pltpu.VMEM((2, 8, LANES), F32),
+            pltpu.VMEM((2, 8, LANES), F32),
+            pltpu.VMEM((8, 8, LANES), F32),
+            pltpu.VMEM((8, 8, LANES), F32),
+            pltpu.VMEM((slots, 24, LANES), F32),
+            pltpu.VMEM((slots, 16, LANES), F32),
             dma((3,)),
             dma((14,)), dma((14,)), dma((14,)), dma((14,)),
-            dma((links,)), dma((links,)), dma((links,)), dma((links,)),
+            dma((slots,)), dma((slots,)), dma((slots,)), dma((slots,)),
         ],
         compiler_params=pltpu.CompilerParams(
             collective_id=0, has_side_effects=True, vmem_limit_bytes=32 * 1024 * 1024),
         name="lanczos",
     )(
-        start_block.reshape(B * 24, LANES),
-        pair_blocks.reshape(9, 16, 8, LANES),
-        slot_map.reshape(16, 8, LANES),
+        pltpu.with_memory_space_constraint(start_block.reshape(B * 24, LANES), pltpu.HBM),
+        pltpu.with_memory_space_constraint(pair_blocks.reshape(9, 16, 8, LANES), pltpu.HBM),
+        pltpu.with_memory_space_constraint(slot_map.reshape(16, 8, LANES), pltpu.HBM),
     )
-    alpha1, alpha2, beta1, beta2, basis3 = results
+    alpha1, alpha2, beta1, beta2, basis3 = pl.pallas_call(
+        deliver,
+        out_shape=tuple(jax.ShapeDtypeStruct(r.shape, F32) for r in results),
+        in_specs=[pl.BlockSpec(memory_space=pl.ANY)] * 5,
+        out_specs=(hbm,) * 5,
+        scratch_shapes=[dma((5,))],
+        compiler_params=pltpu.CompilerParams(vmem_limit_bytes=2 * 1024 * 1024),
+        name="deliver",
+    )(*results)
     return alpha1, alpha2, beta1, beta2, basis3.reshape(start_block.shape)
 
 

time: 82.3 us -> 64 us (0.78)
  Pallas kernels: 75.1 us -> 63.3 us
  local copies, waits for them, and re-layouts: 6.06 us -> 0 us
    pallas_call x1 -> x2, Pallas kernels: 75.1 us -> 63.3 us  [the longest x1 62.4 us: local(): pl.pallas_call(functools.partial(kernel, sizes, row_count, offsets, stage...]
    unnamed x11 -> x0, local copies, waits for them, and re-layouts: 6.06 us -> none
where the time goes in v2:
time: 64 us; the launch traced here: 63.9 us
  Pallas kernels  63.3 us (99%)
  between operations  0.64 us (1%)
    pallas_call x1, Pallas kernels, local(): pl.pallas_call(functools.partial(kernel, sizes, row_count, offsets, stage...  62.4 us

profile of v2, /device:TPU:32, one launch (start us, length us, event | category | flops | bytes accessed | tf_op | source)
XLA Modules:
  0.0 63.9 jit_solution(4590491481036459987)
XLA Ops:
  0.6 62.4 %lanczos.1 = (f32[32,32]{1,0:T(8,128)S(1)}, f32[32,32]{1,0:T(8,128)S(1)}, f32[32,32]{1,0:T(8,128)S(1)}, f32[32,32]{1,0:T(8,128)S(1)}, f32[768,128]{1,0:T(8,128)S(1)}) custom-call(f32[768,128]{1,0:T(8,128)} %bitcast.7, f32[9,16,8,128]{3,2,1,0:T(8,128)} %bitcast.6, s32[16,8,128]{2,1,0:T(8,128)} %bitcast.8), custom_call_target="tpu_custom_call" | custom-call | tf_op jit(solution)/shard_map/lanczos/pallas_call | solution.py:408
  63.1 0.8 %deliver.1 = (f32[32,32]{1,0:T(8,128)}, f32[32,32]{1,0:T(8,128)}, f32[32,32]{1,0:T(8,128)}, f32[32,32]{1,0:T(8,128)}, f32[768,128]{1,0:T(8,128)}) custom-call(f32[32,32]{1,0:T(8,128)S(1)} %get-tuple-element.15.refs_0_, f32[32,32]{1,0:T(8,128)S(1)} %get-tuple-element.16.refs_1_, f32[32,32]{1,0:T(8,128)S(1)} %get-tuple-element.17.refs_2_, ...), custom_call_target="tpu_custom_call" | custom-call | tf_op jit(solution)/shard_map/deliver/pallas_call | solution.py:443

commit v3 on v2

--- a/solution.py
+++ b/solution.py
@@ -44,7 +44,7 @@
     sizes, row_count, offsets, stages, moves,
     start_hbm, pair_hbm, slot_hbm,
     alpha1_ref, alpha2_ref, beta1_ref, beta2_ref, out_ref,
-    start, pair, slot, coup, ext_v, ext_w, u_ref, zm1, zm0, zp0, zp1,
+    start, pair, slot, coup, ext_v, ext_w, u_ref, shares, totals, zm1, zm0, zp0, zp1,
     pack_v, pack_w, edge_v, edge_w, gather1, gather2,
     local_sem, hsend_v, hrecv_v, hsend_w, hrecv_w, rsend1, rrecv1, rsend2, rrecv2,
 ):
@@ -93,8 +93,9 @@
             side = 0 if sign == 1 else 2
             sub = 1 if sign == 1 else 0
             add((sign, 0, 0), ext.at[1, pl.ds(1, 4)], ext.at[side, pl.ds(1, 4)])
-            add((0, sign, 0), ext.at[1, near], ext.at[1, far])
-            add((sign, sign, 0), ext.at[1, near, sub], ext.at[side, far, sub])
+            add((0, sign, 0), ext.at[1, near, sub], ext.at[1, far, sub])
+            add((0, sign, 0), ext.at[1, near, 1 - sub], ext.at[1, far, 1 - sub])
+            add((sign, 0, 0), ext.at[1, far, sub], ext.at[side, far, sub])
             base = 0 if sign == 1 else 4
             src = pack.at[0 if sign == 1 else 1]
             add((0, 0, sign), src, edge.at[base])
@@ -103,8 +104,10 @@
             add((sign, sign, sign), src, edge.at[base + 3])
         return copies
 
-    plane_first = (3, 10, 1, 8, 5, 12)
-    plane_last = (0, 7, 2, 9, 4, 11, 6, 13)
+    send_first = (4, 12, 6, 14, 5, 13, 7, 15, 1, 9, 0, 8, 2, 10)
+    pass_on = ((1, 3), (9, 11))
+    plane_waits = (4, 12, 6, 14, 2, 10)
+    side_waits = (0, 8, 5, 13, 7, 15, 3, 11)
 
     def turn(tile, amount):
         amount = amount % LANES
@@ -269,7 +272,7 @@
     pack_edges(ext_v, pack_v)
     pl.semaphore_wait(barrier, len(offsets) + len(moves))
     halo_v = halo(ext_v, pack_v, edge_v, hsend_v, hrecv_v)
-    for n in (3, 10, 5, 12, 4, 11, 6, 13, 1, 8, 0, 7, 2, 9):
+    for n in send_first:
         halo_v[n].start()
 
     loads[1].wait()
@@ -292,41 +295,74 @@
             coup[DIRECTIONS, i * 3 + j] = -0.5 * (sums[i * 3 + j] + sums[j * 3 + i])
 
     moment0 = gram([v_row], [v_row])
-
-    for n in plane_first:
+    for came, goes in pass_on:
+        halo_v[came].wait_recv()
+        halo_v[goes].start()
+
+    for n in plane_waits:
         halo_v[n].wait_recv()
     shift_plane(ext_v, edge_v)
     apply_terms(plane_terms, ext_v, write_w, None)
-    for n in plane_last:
+    for n in side_waits:
         halo_v[n].wait_recv()
     shift_sides(ext_v, edge_v)
     apply_terms(side_terms, ext_v, write_w, w_row)
 
     pack_edges(ext_w, pack_w)
     halo_w = halo(ext_w, pack_w, edge_w, hsend_w, hrecv_w)
-    for n in (3, 10, 5, 12, 4, 11, 6, 13, 1, 8, 0, 7, 2, 9):
+    for n in send_first:
         halo_w[n].start()
 
+    row_id = lax.broadcasted_iota(jnp.int32, (B, B), 0)
+    lane_id = lax.broadcasted_iota(jnp.int32, (B, B), 1)
+    identity = jnp.where(row_id == lane_id, 1.0, 0.0)
     moments = gram([w_row], [v_row, w_row])
-    sum1 = [reduce_start(0, gather1, packed([moment0, moments[:, :B], moments[:, B:]]), rsend1, rrecv1)]
-
-    for n in plane_first:
+    moment1, moment2 = moments[:, :B], moments[:, B:]
+    diagonal = jnp.sum(jnp.where(row_id == lane_id, moment1, 0.0), axis=0, keepdims=True)
+    corner = jnp.where((row_id == 1) & (lane_id == B - 1), moment1[:1, :1], 0.0)
+    shares[0] = packed([jnp.where(row_id >= lane_id, moment0, moment1)])
+    shares[1] = packed([jnp.where(row_id >= lane_id, moment2, jnp.where(row_id == 0, diagonal, corner))])
+    core = place["core"]
+    other = (me[0] + 1 - 2 * core, me[1], me[2])
+    swap = pltpu.make_async_remote_copy(
+        src_ref=shares.at[1 - core], dst_ref=gather1.at[0], send_sem=rsend1.at[0], recv_sem=rrecv1.at[0],
+        device_id=other, device_id_type=MESH)
+    swap.start()
+    swap.wait_recv()
+    sum1 = [reduce_start(1, gather1, shares[core] + gather1[0], rsend1, rrecv1)]
+    for came, goes in pass_on:
+        halo_w[came].wait_recv()
+        halo_w[goes].start()
+
+    for n in plane_waits:
         halo_w[n].wait_recv()
     shift_plane(ext_w, edge_w)
-    total = reduce_finish(0, gather1, sum1[0])
-    sum1.append(reduce_start(1, gather1, total, rsend1, rrecv1))
+    total = reduce_finish(1, gather1, sum1[0])
+    sum1.append(reduce_start(2, gather1, total, rsend1, rrecv1))
     apply_terms(plane_terms, ext_w, write_u, None)
-    total = reduce_finish(1, gather1, sum1[1])
-    sum1.append(reduce_start(2, gather1, total, rsend1, rrecv1))
-    for n in plane_last:
+    totals[core] = reduce_finish(2, gather1, sum1[1]) * (1.0 / row_count)
+    swap_back = pltpu.make_async_remote_copy(
+        src_ref=totals.at[core], dst_ref=totals.at[core], send_sem=rsend1.at[1], recv_sem=rrecv1.at[1],
+        device_id=other, device_id_type=MESH)
+    swap_back.start()
+    sum1.append([swap, swap_back])
+    for n in side_waits:
         halo_w[n].wait_recv()
     shift_sides(ext_w, edge_w)
     apply_terms(side_terms, ext_w, write_u, u_row)
 
     moments = gram([u_row], [w_row, u_row])
     sum2 = [reduce_start(0, gather2, packed([moments[:, :B], moments[:, B:]]), rsend2, rrecv2)]
-    first = reduce_finish(2, gather1, sum1[2]) * (1.0 / row_count)
-    m0, m1, m2 = unpacked(first[:8]), unpacked(first[8:16]), unpacked(first[16:])
+    swap_back.wait_recv()
+
+    def mirrored(half):
+        return half + mt(identity, jnp.where(row_id == lane_id, 0.0, half))
+
+    one, two = unpacked(totals[0]), unpacked(totals[1])
+    m0 = mirrored(jnp.where(row_id >= lane_id, one, 0.0))
+    m2 = mirrored(jnp.where(row_id >= lane_id, two, 0.0))
+    diagonal = jnp.where(lane_id == 0, two[1:2, B - 1 :], two[:1, :])
+    m1 = mirrored(jnp.where(row_id < lane_id, one, jnp.where(row_id == lane_id, diagonal, 0.0)))
     total = reduce_finish(0, gather2, sum2[0])
     sum2.append(reduce_start(1, gather2, total, rsend2, rrecv2))
 
@@ -418,6 +454,8 @@
             extended,
             extended,
             pltpu.VMEM((4, 2, 3, B, LANES), F32),
+            pltpu.VMEM((2, 8, LANES), F32),
+            pltpu.VMEM((2, 8, LANES), F32),
             pltpu.VMEM((2, 5, 3, B, LANES), F32),
             pltpu.VMEM((4, 3, B, LANES), F32),
             pltpu.VMEM((2, 5, 3, B, LANES), F32),
@@ -426,10 +464,10 @@
             pltpu.VMEM((2, 8, LANES), F32),
             pltpu.VMEM((8, 8, LANES), F32),
             pltpu.VMEM((8, 8, LANES), F32),
-            pltpu.VMEM((slots, 24, LANES), F32),
+            pltpu.VMEM((slots, 8, LANES), F32),
             pltpu.VMEM((slots, 16, LANES), F32),
             dma((3,)),
-            dma((14,)), dma((14,)), dma((14,)), dma((14,)),
+            dma((16,)), dma((16,)), dma((16,)), dma((16,)),
             dma((slots,)), dma((slots,)), dma((slots,)), dma((slots,)),
         ],
         compiler_params=pltpu.CompilerParams(

time: 64 us -> 61.3 us (0.958); the launches traced: 63.9 us -> 60.5 us
  Pallas kernels: 63.3 us -> 59.9 us
    pallas_call x1, Pallas kernels: 62.4 us -> 59.1 us  [local(): pl.pallas_call(functools.partial(kernel, sizes, row_count, offsets, stage...]
where the time goes in v3:
time: 61.3 us; the launch traced here: 60.5 us
  Pallas kernels  59.9 us (98%)
  between operations  0.64 us (1%)
    pallas_call x1, Pallas kernels, local(): pl.pallas_call(functools.partial(kernel, sizes, row_count, offsets, stage...  59.1 us

profile of v3, /device:TPU:32, one launch (start us, length us, event | category | flops | bytes accessed | tf_op | source)
XLA Modules:
  0.0 60.5 jit_solution(17680837323592565048)
XLA Ops:
  0.6 59.1 %lanczos.1 = (f32[32,32]{1,0:T(8,128)S(1)}, f32[32,32]{1,0:T(8,128)S(1)}, f32[32,32]{1,0:T(8,128)S(1)}, f32[32,32]{1,0:T(8,128)S(1)}, f32[768,128]{1,0:T(8,128)S(1)}) custom-call(f32[768,128]{1,0:T(8,128)} %bitcast.7, f32[9,16,8,128]{3,2,1,0:T(8,128)} %bitcast.6, s32[16,8,128]{2,1,0:T(8,128)} %bitcast.8), custom_call_target="tpu_custom_call" | custom-call | tf_op jit(solution)/shard_map/lanczos/pallas_call | solution.py:444
  59.7 0.8 %deliver.1 = (f32[32,32]{1,0:T(8,128)}, f32[32,32]{1,0:T(8,128)}, f32[32,32]{1,0:T(8,128)}, f32[32,32]{1,0:T(8,128)}, f32[768,128]{1,0:T(8,128)}) custom-call(f32[32,32]{1,0:T(8,128)S(1)} %get-tuple-element.15.refs_0_, f32[32,32]{1,0:T(8,128)S(1)} %get-tuple-element.16.refs_1_, f32[32,32]{1,0:T(8,128)S(1)} %get-tuple-element.17.refs_2_, ...), custom_call_target="tpu_custom_call" | custom-call | tf_op jit(solution)/shard_map/deliver/pallas_call | solution.py:481

commit v4 on v3

--- a/solution.py
+++ b/solution.py
@@ -28,16 +28,22 @@
 
 
 def factor(gram):
-    row_id = lax.broadcasted_iota(jnp.int32, (B, 2 * B), 0)
-    lane_id = lax.broadcasted_iota(jnp.int32, (B, 2 * B), 1)
-    work = jnp.concatenate([gram, jnp.where(row_id == lane_id, 1.0, 0.0)[:, :B].astype(F32)], axis=1)
-    for k in range(B - 1):
-        scaled = work[:, k : k + 1] / work[k : k + 1, k : k + 1]
-        work = work - jnp.where(row_id > k, scaled * work[k : k + 1, :], 0.0)
-    diagonal = jnp.sum(jnp.where(row_id == lane_id, work, 0.0), axis=1, keepdims=True)
-    work = work * (1.0 / jnp.sqrt(diagonal))
-    upper = jnp.where(row_id <= lane_id, work, 0.0)[:, :B]
-    return upper.T, upper, work[:, B:]
+    row_id = lax.broadcasted_iota(jnp.int32, (B, LANES), 0)
+    lane_id = lax.broadcasted_iota(jnp.int32, (B, LANES), 1)
+    columns = [jnp.broadcast_to(gram[:, j : j + 1], (B, LANES)) for j in range(B)]
+    inverse = jnp.where(row_id == lane_id, 1.0, 0.0).astype(F32)
+    lower = jnp.zeros((B, LANES), F32)
+    for k in range(B):
+        scale = 1.0 / jnp.sqrt(columns[k][k : k + 1])
+        column = jnp.where(row_id >= k, columns[k] * scale, 0.0)
+        lower = jnp.where(lane_id == k, column, lower)
+        for j in range(k + 1, B):
+            top = j // 8 * 8
+            rest = columns[j][top:] - column[top:] * column[j : j + 1]
+            columns[j] = jnp.concatenate([columns[j][:top], rest], axis=0) if top else rest
+        row = inverse[k : k + 1] * scale
+        inverse = jnp.where(row_id > k, inverse - column * row, jnp.where(row_id == k, row, inverse))
+    return lower[:, :B], inverse[:, :B]
 
 
 def kernel(
@@ -366,17 +372,18 @@
     total = reduce_finish(0, gather2, sum2[0])
     sum2.append(reduce_start(1, gather2, total, rsend2, rrecv2))
 
-    _, _, inverse0 = factor(m0)
+    _, inverse0 = factor(m0)
 
     alpha1 = mt(mm(inverse0, m1), inverse0)
     square1 = mt(mm(inverse0, m2), inverse0)
     total = reduce_finish(1, gather2, sum2[1])
     sum2.append(reduce_start(2, gather2, total, rsend2, rrecv2))
 
-    beta1, upper1, inverse1 = factor(square1 - mt(alpha1, alpha1))
+    beta1, inverse1 = factor(square1 - mt(alpha1, alpha1))
 
     on_w = mm(inverse1, inverse0)
     on_v = -mm(mm(inverse1, alpha1), inverse0)
+    upper1 = mt(identity, beta1)
     on_m2 = mm(on_v, m2)
     known_alpha = mt(on_m2, on_w) + mt(on_w, on_m2) + mt(mm(on_v, m1), on_v)
     known_square = mt(on_m2, on_v) - mt(upper1, upper1)
@@ -387,7 +394,7 @@
     on_m3 = mm(on_w, m3)
     alpha2 = mt(on_m3, on_w) + known_alpha
     square2 = (mt(mm(on_w, m4), on_w) + mt(on_m3, on_v)) + (mt(on_v, on_m3) + known_square)
-    beta2, _, inverse2 = factor(square2 - mt(alpha2, alpha2))
+    beta2, inverse2 = factor(square2 - mt(alpha2, alpha2))
 
     weights = jnp.concatenate(
         [-(mm(alpha2, on_v) + from_v), on_v - mm(alpha2, on_w), on_w], axis=1)

time: 61.3 us -> 55.4 us (0.904)
  Pallas kernels: 59.9 us -> 54 us
    pallas_call x1, Pallas kernels: 59.1 us -> 53.2 us  [local(): pl.pallas_call(functools.partial(kernel, sizes, row_count, offsets, stage...]
where the time goes in v4:
time: 55.4 us; the launch traced here: 54.7 us
  Pallas kernels  54 us (97%)
  between operations  0.64 us (1%)
    pallas_call x1, Pallas kernels, local(): pl.pallas_call(functools.partial(kernel, sizes, row_count, offsets, stage...  53.2 us

profile of v4, /device:TPU:32, one launch (start us, length us, event | category | flops | bytes accessed | tf_op | source)
XLA Modules:
  0.0 54.7 jit_solution(15964234949811000852)
XLA Ops:
  0.6 53.2 %lanczos.1 = (f32[32,32]{1,0:T(8,128)S(1)}, f32[32,32]{1,0:T(8,128)S(1)}, f32[32,32]{1,0:T(8,128)S(1)}, f32[32,32]{1,0:T(8,128)S(1)}, f32[768,128]{1,0:T(8,128)S(1)}) custom-call(f32[768,128]{1,0:T(8,128)} %bitcast.7, f32[9,16,8,128]{3,2,1,0:T(8,128)} %bitcast.6, s32[16,8,128]{2,1,0:T(8,128)} %bitcast.8), custom_call_target="tpu_custom_call" | custom-call | tf_op jit(solution)/shard_map/lanczos/pallas_call | solution.py:451
  53.9 0.8 %deliver.1 = (f32[32,32]{1,0:T(8,128)}, f32[32,32]{1,0:T(8,128)}, f32[32,32]{1,0:T(8,128)}, f32[32,32]{1,0:T(8,128)}, f32[768,128]{1,0:T(8,128)}) custom-call(f32[32,32]{1,0:T(8,128)S(1)} %get-tuple-element.15.refs_0_, f32[32,32]{1,0:T(8,128)S(1)} %get-tuple-element.16.refs_1_, f32[32,32]{1,0:T(8,128)S(1)} %get-tuple-element.17.refs_2_, ...), custom_call_target="tpu_custom_call" | custom-call | tf_op jit(solution)/shard_map/deliver/pallas_call | solution.py:488

commit v5 on v4

--- a/solution.py
+++ b/solution.py
@@ -340,25 +340,27 @@
         halo_w[came].wait_recv()
         halo_w[goes].start()
 
+    total = reduce_finish(1, gather1, sum1[0])
+    sum1.append(reduce_start(2, gather1, total, rsend1, rrecv1))
     for n in plane_waits:
         halo_w[n].wait_recv()
     shift_plane(ext_w, edge_w)
-    total = reduce_finish(1, gather1, sum1[0])
-    sum1.append(reduce_start(2, gather1, total, rsend1, rrecv1))
     apply_terms(plane_terms, ext_w, write_u, None)
+    for n in side_waits:
+        halo_w[n].wait_recv()
+    shift_sides(ext_w, edge_w)
+    apply_terms(side_terms, ext_w, write_u, u_row)
+
+    moments = gram([u_row], [w_row, u_row])
+    sum2 = [reduce_start(0, gather2, packed([moments[:, :B], moments[:, B:]]), rsend2, rrecv2)]
     totals[core] = reduce_finish(2, gather1, sum1[1]) * (1.0 / row_count)
     swap_back = pltpu.make_async_remote_copy(
         src_ref=totals.at[core], dst_ref=totals.at[core], send_sem=rsend1.at[1], recv_sem=rrecv1.at[1],
         device_id=other, device_id_type=MESH)
     swap_back.start()
     sum1.append([swap, swap_back])
-    for n in side_waits:
-        halo_w[n].wait_recv()
-    shift_sides(ext_w, edge_w)
-    apply_terms(side_terms, ext_w, write_u, u_row)
-
-    moments = gram([u_row], [w_row, u_row])
-    sum2 = [reduce_start(0, gather2, packed([moments[:, :B], moments[:, B:]]), rsend2, rrecv2)]
+    total = reduce_finish(0, gather2, sum2[0])
+    sum2.append(reduce_start(1, gather2, total, rsend2, rrecv2))
     swap_back.wait_recv()
 
     def mirrored(half):
@@ -369,9 +371,6 @@
     m2 = mirrored(jnp.where(row_id >= lane_id, two, 0.0))
     diagonal = jnp.where(lane_id == 0, two[1:2, B - 1 :], two[:1, :])
     m1 = mirrored(jnp.where(row_id < lane_id, one, jnp.where(row_id == lane_id, diagonal, 0.0)))
-    total = reduce_finish(0, gather2, sum2[0])
-    sum2.append(reduce_start(1, gather2, total, rsend2, rrecv2))
-
     _, inverse0 = factor(m0)
 
     alpha1 = mt(mm(inverse0, m1), inverse0)
@@ -442,7 +441,8 @@
             span *= DIGITS[digit]
         stages.append({"digits": digits, "moves": steps, "stride": stride, "slot": slots})
         slots += len(steps)
-        moves += [(len(stages) - 1, step) for step in steps[1:]]
+        if digits != ("core",):
+            moves += [(len(stages) - 1, step) for step in steps[1:]]
     dma = pltpu.SemaphoreType.DMA
     small = jax.ShapeDtypeStruct((B, B), F32)
     vmem = pl.BlockSpec(memory_space=pltpu.VMEM)

time: 55.4 us -> 50.9 us (0.919); the launches traced: 54.7 us -> 50.7 us
  Pallas kernels: 54 us -> 50.1 us
    pallas_call x1, Pallas kernels: 53.2 us -> 49.3 us  [local(): pl.pallas_call(functools.partial(kernel, sizes, row_count, offsets, stage...]
where the time goes in v5:
time: 50.9 us; the launch traced here: 50.7 us
  Pallas kernels  50.1 us (98%)
  between operations  0.64 us (1%)
    pallas_call x1, Pallas kernels, local(): pl.pallas_call(functools.partial(kernel, sizes, row_count, offsets, stage...  49.3 us

profile of v5, /device:TPU:32, one launch (start us, length us, event | category | flops | bytes accessed | tf_op | source)
XLA Modules:
  0.0 50.7 jit_solution(12626786573961336580)
XLA Ops:
  0.6 49.3 %lanczos.1 = (f32[32,32]{1,0:T(8,128)S(1)}, f32[32,32]{1,0:T(8,128)S(1)}, f32[32,32]{1,0:T(8,128)S(1)}, f32[32,32]{1,0:T(8,128)S(1)}, f32[768,128]{1,0:T(8,128)S(1)}) custom-call(f32[768,128]{1,0:T(8,128)} %bitcast.7, f32[9,16,8,128]{3,2,1,0:T(8,128)} %bitcast.6, s32[16,8,128]{2,1,0:T(8,128)} %bitcast.8), custom_call_target="tpu_custom_call" | custom-call | tf_op jit(solution)/shard_map/lanczos/pallas_call | solution.py:451
  49.9 0.8 %deliver.1 = (f32[32,32]{1,0:T(8,128)}, f32[32,32]{1,0:T(8,128)}, f32[32,32]{1,0:T(8,128)}, f32[32,32]{1,0:T(8,128)}, f32[768,128]{1,0:T(8,128)}) custom-call(f32[32,32]{1,0:T(8,128)S(1)} %get-tuple-element.15.refs_0_, f32[32,32]{1,0:T(8,128)S(1)} %get-tuple-element.16.refs_1_, f32[32,32]{1,0:T(8,128)S(1)} %get-tuple-element.17.refs_2_, ...), custom_call_target="tpu_custom_call" | custom-call | tf_op jit(solution)/shard_map/deliver/pallas_call | solution.py:488

commit v6 on v5

--- a/solution.py
+++ b/solution.py
@@ -110,10 +110,13 @@
             add((sign, sign, sign), src, edge.at[base + 3])
         return copies
 
-    send_first = (4, 12, 6, 14, 5, 13, 7, 15, 1, 9, 0, 8, 2, 10)
+    send_first = (4, 12, 6, 14, 5, 13, 7, 15)
+    send_next = (1, 9, 0, 8, 2, 10)
     pass_on = ((1, 3), (9, 11))
-    plane_waits = (4, 12, 6, 14, 2, 10)
-    side_waits = (0, 8, 5, 13, 7, 15, 3, 11)
+    tile_waits = (4, 12, 6, 14)
+    plane_waits = (2, 10)
+    side_waits = (0, 8, 5, 13)
+    edge_waits = (3, 11, 7, 15)
 
     def turn(tile, amount):
         amount = amount % LANES
@@ -159,6 +162,9 @@
                 k = y * 6 + c
                 down(zm1, (0, y + 1, c), ext, (0, 1 + y, 1, c), edge[1], k + 3)
                 up(zp0, (1, y, c), ext, (2, 1 + y, 0, c), edge[5], k)
+
+    def shift_edges(ext, edge):
+        for c in range(3):
             down(zm1, (0, 0, c), ext, (0, 0, 1, c), edge[3], 21 + c)
             up(zp0, (1, 4, c), ext, (2, 5, 0, c), edge[7], c)
 
@@ -195,9 +201,10 @@
         terms.append((9, ext, (0, 1 + y, sub)))
         return terms
 
-    def apply_terms(terms_of, ext, write, read):
-        def body(y, carry):
+    def apply_terms(terms_of, ext, write, read, steps=(0, 4)):
+        def body(step, carry):
             for sub in range(2):
+                y = step if sub else 3 - step
                 total = [read(y, sub, i) if read else jnp.zeros((B, LANES), F32) for i in range(3)]
                 for o, ref, index in terms_of(ext, sub, y):
                     for j in range(3):
@@ -209,7 +216,7 @@
                     write(y, sub, i, total[i])
             return carry
 
-        lax.fori_loop(0, 4, body, 0)
+        lax.fori_loop(*steps, body, 0)
 
     def wide(rows_of, y):
         return jnp.concatenate([rows_of(y, sc // 3, sc % 3) for sc in range(6)], axis=1)
@@ -278,7 +285,7 @@
     pack_edges(ext_v, pack_v)
     pl.semaphore_wait(barrier, len(offsets) + len(moves))
     halo_v = halo(ext_v, pack_v, edge_v, hsend_v, hrecv_v)
-    for n in send_first:
+    for n in send_first + send_next:
         halo_v[n].start()
 
     loads[1].wait()
@@ -305,18 +312,24 @@
         halo_v[came].wait_recv()
         halo_v[goes].start()
 
+    for n in tile_waits:
+        halo_v[n].wait_recv()
+    shift_plane(ext_v, edge_v)
     for n in plane_waits:
         halo_v[n].wait_recv()
-    shift_plane(ext_v, edge_v)
     apply_terms(plane_terms, ext_v, write_w, None)
     for n in side_waits:
         halo_v[n].wait_recv()
     shift_sides(ext_v, edge_v)
-    apply_terms(side_terms, ext_v, write_w, w_row)
+    apply_terms(side_terms, ext_v, write_w, w_row, (0, 3))
+    for n in edge_waits:
+        halo_v[n].wait_recv()
+    shift_edges(ext_v, edge_v)
+    apply_terms(side_terms, ext_v, write_w, w_row, (3, 4))
 
     pack_edges(ext_w, pack_w)
     halo_w = halo(ext_w, pack_w, edge_w, hsend_w, hrecv_w)
-    for n in send_first:
+    for n in send_first + send_next:
         halo_w[n].start()
 
     row_id = lax.broadcasted_iota(jnp.int32, (B, B), 0)
@@ -342,14 +355,20 @@
 
     total = reduce_finish(1, gather1, sum1[0])
     sum1.append(reduce_start(2, gather1, total, rsend1, rrecv1))
+    for n in tile_waits:
+        halo_w[n].wait_recv()
+    shift_plane(ext_w, edge_w)
     for n in plane_waits:
         halo_w[n].wait_recv()
-    shift_plane(ext_w, edge_w)
     apply_terms(plane_terms, ext_w, write_u, None)
     for n in side_waits:
         halo_w[n].wait_recv()
     shift_sides(ext_w, edge_w)
-    apply_terms(side_terms, ext_w, write_u, u_row)
+    apply_terms(side_terms, ext_w, write_u, u_row, (0, 3))
+    for n in edge_waits:
+        halo_w[n].wait_recv()
+    shift_edges(ext_w, edge_w)
+    apply_terms(side_terms, ext_w, write_u, u_row, (3, 4))
 
     moments = gram([u_row], [w_row, u_row])
     sum2 = [reduce_start(0, gather2, packed([moments[:, :B], moments[:, B:]]), rsend2, rrecv2)]

time: 50.9 us -> 50.3 us (0.988)
  Pallas kernels: 50.1 us -> 49.4 us
    pallas_call x1, Pallas kernels: 49.3 us -> 48.6 us  [local(): pl.pallas_call(functools.partial(kernel, sizes, row_count, offsets, stage...]
where the time goes in v6:
time: 50.3 us; the launch traced here: 50 us
  Pallas kernels  49.4 us (98%)
  between operations  0.64 us (1%)
    pallas_call x1, Pallas kernels, local(): pl.pallas_call(functools.partial(kernel, sizes, row_count, offsets, stage...  48.6 us

profile of v6, /device:TPU:32, one launch (start us, length us, event | category | flops | bytes accessed | tf_op | source)
XLA Modules:
  0.0 50.0 jit_solution(14517953313128451911)
XLA Ops:
  0.6 48.6 %lanczos.1 = (f32[32,32]{1,0:T(8,128)S(1)}, f32[32,32]{1,0:T(8,128)S(1)}, f32[32,32]{1,0:T(8,128)S(1)}, f32[32,32]{1,0:T(8,128)S(1)}, f32[768,128]{1,0:T(8,128)S(1)}) custom-call(f32[768,128]{1,0:T(8,128)} %bitcast.7, f32[9,16,8,128]{3,2,1,0:T(8,128)} %bitcast.6, s32[16,8,128]{2,1,0:T(8,128)} %bitcast.8), custom_call_target="tpu_custom_call" | custom-call | tf_op jit(solution)/shard_map/lanczos/pallas_call | solution.py:470
  49.2 0.8 %deliver.1 = (f32[32,32]{1,0:T(8,128)}, f32[32,32]{1,0:T(8,128)}, f32[32,32]{1,0:T(8,128)}, f32[32,32]{1,0:T(8,128)}, f32[768,128]{1,0:T(8,128)}) custom-call(f32[32,32]{1,0:T(8,128)S(1)} %get-tuple-element.15.refs_0_, f32[32,32]{1,0:T(8,128)S(1)} %get-tuple-element.16.refs_1_, f32[32,32]{1,0:T(8,128)S(1)} %get-tuple-element.17.refs_2_, ...), custom_call_target="tpu_custom_call" | custom-call | tf_op jit(solution)/shard_map/deliver/pallas_call | solution.py:507

commit v7 on v6

--- a/solution.py
+++ b/solution.py
@@ -237,12 +237,12 @@
         u_ref[y, s, c] = value
 
     def gram(lefts, rights):
-        def body(y, carry):
+        parts = []
+        for y in range(4):
             right = jnp.concatenate([wide(rows, y) for rows in rights], axis=0)
             left = jnp.concatenate([wide(rows, y) for rows in lefts], axis=0)
-            return carry + mt(left, right)
-
-        return lax.fori_loop(0, 4, body, jnp.zeros((B * len(lefts), B * len(rights)), F32))
+            parts.append(mt(left, right))
+        return (parts[0] + parts[1]) + (parts[2] + parts[3])
 
     def reduce_start(stage, gather, value, send, recv):
         first, count = stages[stage]["slot"], len(stages[stage]["moves"])
@@ -391,11 +391,11 @@
     diagonal = jnp.where(lane_id == 0, two[1:2, B - 1 :], two[:1, :])
     m1 = mirrored(jnp.where(row_id < lane_id, one, jnp.where(row_id == lane_id, diagonal, 0.0)))
     _, inverse0 = factor(m0)
+    total = reduce_finish(1, gather2, sum2[1])
+    sum2.append(reduce_start(2, gather2, total, rsend2, rrecv2))
 
     alpha1 = mt(mm(inverse0, m1), inverse0)
     square1 = mt(mm(inverse0, m2), inverse0)
-    total = reduce_finish(1, gather2, sum2[1])
-    sum2.append(reduce_start(2, gather2, total, rsend2, rrecv2))
 
     beta1, inverse1 = factor(square1 - mt(alpha1, alpha1))
 
@@ -461,7 +461,8 @@
         stages.append({"digits": digits, "moves": steps, "stride": stride, "slot": slots})
         slots += len(steps)
         if digits != ("core",):
-            moves += [(len(stages) - 1, step) for step in steps[1:]]
+            near = ((1, 0), (DIGITS["z_lo"] - 1, 0)) if digits[0] == "z_lo" else ()
+            moves += [(len(stages) - 1, step) for step in steps[1:] if step not in near]
     dma = pltpu.SemaphoreType.DMA
     small = jax.ShapeDtypeStruct((B, B), F32)
     vmem = pl.BlockSpec(memory_space=pltpu.VMEM)

time: 50.3 us -> 50.9 us (1.012)
  Pallas kernels: 49.4 us -> 50 us
    pallas_call x1, Pallas kernels: 48.6 us -> 49.2 us  [local(): pl.pallas_call(functools.partial(kernel, sizes, row_count, offsets, stage...]
where the time goes in v7:
time: 50.9 us; the launch traced here: 50.6 us
  Pallas kernels  50 us (98%)
  between operations  0.64 us (1%)
    pallas_call x1, Pallas kernels, local(): pl.pallas_call(functools.partial(kernel, sizes, row_count, offsets, stage...  49.2 us

profile of v7, /device:TPU:32, one launch (start us, length us, event | category | flops | bytes accessed | tf_op | source)
XLA Modules:
  0.0 50.6 jit_solution(4848006778604114254)
XLA Ops:
  0.6 49.2 %lanczos.1 = (f32[32,32]{1,0:T(8,128)S(1)}, f32[32,32]{1,0:T(8,128)S(1)}, f32[32,32]{1,0:T(8,128)S(1)}, f32[32,32]{1,0:T(8,128)S(1)}, f32[768,128]{1,0:T(8,128)S(1)}) custom-call(f32[768,128]{1,0:T(8,128)} %bitcast.7, f32[9,16,8,128]{3,2,1,0:T(8,128)} %bitcast.6, s32[16,8,128]{2,1,0:T(8,128)} %bitcast.8), custom_call_target="tpu_custom_call" | custom-call | tf_op jit(solution)/shard_map/lanczos/pallas_call | solution.py:471
  49.8 0.8 %deliver.1 = (f32[32,32]{1,0:T(8,128)}, f32[32,32]{1,0:T(8,128)}, f32[32,32]{1,0:T(8,128)}, f32[32,32]{1,0:T(8,128)}, f32[768,128]{1,0:T(8,128)}) custom-call(f32[32,32]{1,0:T(8,128)S(1)} %get-tuple-element.15.refs_0_, f32[32,32]{1,0:T(8,128)S(1)} %get-tuple-element.16.refs_1_, f32[32,32]{1,0:T(8,128)S(1)} %get-tuple-element.17.refs_2_, ...), custom_call_target="tpu_custom_call" | custom-call | tf_op jit(solution)/shard_map/deliver/pallas_call | solution.py:508
